TPU v7x, 256 devices: a whole 4x4x8 slice. The times are simulated.
256 devices in a mesh: grp: 4 (over z_lo, core), tp: 64 (over y, x, z_hi).
Axes of the slice: x: 4, y: 4, z: 8 (z_hi: 4, z_lo: 2; z = z_hi * 2 + z_lo), core: 2. Of those that a mesh axis runs over, the one named last changes fastest.
Arguments:
- hidden: bfloat16 [32768, 1024], P(('grp', 'tp')), may hold values from -6 to 6
- ln_gain: bfloat16 [1024], replicated, may hold values from 0.5 to 1.5
- w_query: bfloat16 [1024, 1024], replicated, may hold values from -0.1875 to 0.1875
- w_key: bfloat16 [1024, 1024], replicated, may hold values from -0.1875 to 0.1875
- w_value: bfloat16 [1024, 1024], replicated, may hold values from -0.1875 to 0.1875
- w_out: bfloat16 [1024, 1024], replicated, may hold values from -0.1875 to 0.1875
- rel_bias: float32 [32, 16], replicated, may hold values from -8 to 8
- prefix_cache: bfloat16 [8, 512, 2, 1024], P('grp', 'tp'), may hold values from -14 to 14
- bucket_of_distance: int32 [1024], replicated, may hold values from 0 to 31, never falling along the last dimension, each value on 1 to 256 neighbouring positions
- slot_of_group: int32 [8], replicated, may hold values from 0 to 7, each once
- suffix_lengths: int32 [4, 128], P('grp'), may hold values from 1 to 512, 8192 in all within a row
- request_group: int32 [4, 128], P('grp'), may hold values from 0 to 1
Outputs:
- attended: bfloat16 [32768, 1024], P(('grp', 'tp'))
Inputs may be any that keep to these rules, and one draw needn't show every extreme that they name: `suffix_lengths`: each row's lengths sum to 8192; the longest is exactly 512. `slot_of_group`: every slot holds exactly one group. `bucket_of_distance`: never falls with the distance; bucket 0 starts at distance 0.
All inputs are finite; a program needn't handle non-finite values.
Results may differ from a plain program's by a relative error of at most 0.005.
The roundings to bfloat16 on the way count: a program that leaves them out, or rounds other values in their place, can miss the bound.
Values may be sent and summed in bfloat16 or wider, within the bound.
A program may use at most 192 MiB of HBM per device.

v0:
```python
import jax
import jax.numpy as jnp
from jax import lax
from jax.sharding import PartitionSpec as P

PREFIX = 512
GRP_SLOTS = 2
LMAX = 512


def shifted(array, axis, by):
    peers = lax.axis_size(axis)
    pairs = [(i, i + by) for i in range(peers) if 0 <= i + by < peers]
    return lax.ppermute(array, axis, pairs)


def request_meta(lens, rows):
    ends = jnp.cumsum(lens)
    starts = ends - lens
    count = lens.shape[0]
    req = jnp.sum((rows[:, None] >= ends[None, :]).astype(jnp.int32), axis=1)
    req = jnp.minimum(req, count - 1)
    onehot = req[:, None] == jnp.arange(count)[None, :]
    start_of = jnp.sum(jnp.where(onehot, starts[None, :], 0), axis=1)
    return (req, rows - start_of, onehot)


def shards(
    hidden,
    ln_gain,
    w_query,
    w_key,
    w_value,
    w_out,
    rel_bias,
    prefix_cache,
    bucket_of_distance,
    slot_of_group,
    suffix_lengths,
    request_group,
):
    tok, width = hidden.shape
    heads = rel_bias.shape[1]
    head_dim = width // heads
    tp_index = lax.axis_index("tp")
    row_index = lax.axis_index("grp")
    x = hidden.astype(jnp.float32)
    normed = (
        x * lax.rsqrt(jnp.mean(x * x, axis=1, keepdims=True) + 1e-06) * ln_gain.astype(jnp.float32)
    ).astype(jnp.bfloat16)
    query = jnp.dot(normed, w_query, preferred_element_type=jnp.float32).astype(jnp.bfloat16)
    key = jnp.dot(normed, w_key, preferred_element_type=jnp.float32).astype(jnp.bfloat16)
    value = jnp.dot(normed, w_value, preferred_element_type=jnp.float32).astype(jnp.bfloat16)
    buckets = rel_bias.shape[0]
    table = jnp.dot(
        jax.nn.one_hot(bucket_of_distance, buckets, dtype=jnp.float32),
        rel_bias,
        precision=lax.Precision.HIGHEST,
    )
    table_heads = table.T
    span = table.shape[0]
    lens = suffix_lengths[0]
    groups = request_group[0]
    reach = LMAX // tok

    def block_meta(block):
        rows = block * tok + jnp.arange(tok)
        req, pos, onehot = request_meta(lens, rows)
        req = jnp.where(rows >= 0, req, -1)
        return (req, pos, onehot)

    my_req, my_pos, my_onehot = block_meta(tp_index)
    my_group = jnp.sum(jnp.where(my_onehot, groups[None, :], 0), axis=1)
    slot_pick = (my_group[:, None] == jnp.arange(GRP_SLOTS)[None, :]).astype(jnp.float32)
    packed = jnp.stack([key, value], axis=1)
    earlier = []
    for step in range(1, reach + 1):
        earlier.append(shifted(packed, "tp", step))
    keys_all = jnp.concatenate(earlier[::-1] + [packed], axis=0)
    metas = [block_meta(tp_index - back) for back in range(reach, -1, -1)]
    req_keys = jnp.concatenate([item[0] for item in metas], axis=0)
    pos_keys = jnp.concatenate([item[1] for item in metas], axis=0)
    query_heads = query.reshape(tok, heads, head_dim)
    key_heads = keys_all[:, 0].reshape(-1, heads, head_dim)
    value_heads = keys_all[:, 1].reshape(-1, heads, head_dim)
    dist = jnp.clip(my_pos[:, None] - pos_keys[None, :], 0, span - 1)
    scores = jnp.einsum("qhd,khd->hqk", query_heads, key_heads, preferred_element_type=jnp.float32)
    scores = scores + table_heads[:, dist]
    valid = (my_req[:, None] == req_keys[None, :]) & (pos_keys[None, :] <= my_pos[:, None])
    scores = jnp.where(valid[None, :, :], scores, -jnp.inf)
    top = jnp.max(scores, axis=-1)
    probs = jnp.exp(scores - top[..., None])
    total = jnp.sum(probs, axis=-1)
    mixed = jnp.einsum(
        "hqk,khd->qhd", probs.astype(jnp.bfloat16), value_heads, preferred_element_type=jnp.float32
    )
    row_slots = lax.dynamic_slice_in_dim(slot_of_group, row_index * GRP_SLOTS, GRP_SLOTS)
    owners = lax.all_gather(prefix_cache, "grp", axis=0, tiled=True)
    rows_kv = jnp.take(lax.all_gather(owners, "tp", axis=1, tiled=True), row_slots, axis=0)
    best = top
    summed = total
    gathered = mixed
    slots_here = rows_kv.shape[0]
    count = rows_kv.shape[1]
    key_pos = jnp.arange(count)
    dist_pre = PREFIX + my_pos[:, None] - key_pos[None, :]
    keys_cat = rows_kv[:, :, 0].reshape(slots_here * count, heads, head_dim)
    values_cat = rows_kv[:, :, 1].reshape(slots_here * count, heads, head_dim)
    s_all = jnp.einsum("qhd,khd->hqk", query_heads, keys_cat, preferred_element_type=jnp.float32)
    s_all = s_all.reshape(heads, tok, slots_here, count)
    fresh = jnp.sum(s_all * slot_pick[None, :, :, None], axis=2)
    fresh = fresh + table_heads[:, dist_pre]
    best_new = jnp.maximum(best, jnp.max(fresh, axis=-1))
    factor = jnp.exp(best - best_new)
    weights = jnp.exp(fresh - best_new[..., None])
    summed = summed * factor + jnp.sum(weights, axis=-1)
    rounded = weights.astype(jnp.bfloat16)
    picked = (rounded[:, :, None, :] * slot_pick.astype(jnp.bfloat16)[None, :, :, None]).reshape(
        heads, tok, slots_here * count
    )
    gathered = gathered * factor.T[..., None] + jnp.einsum(
        "hqk,khd->qhd", picked, values_cat, preferred_element_type=jnp.float32
    )
    carry = (best_new, summed, gathered)
    best, summed, gathered = carry
    result = (gathered / summed.T[..., None]).reshape(tok, width).astype(jnp.bfloat16)
    return jnp.dot(result, w_out, preferred_element_type=jnp.float32).astype(jnp.bfloat16)


def solution(mesh):
    in_specs = (
        P(("grp", "tp"), None),
        P(),
        P(),
        P(),
        P(),
        P(),
        P(),
        P("grp", "tp", None, None),
        P(),
        P(),
        P("grp", None),
        P("grp", None),
    )
    out_specs = P(("grp", "tp"), None)
    return jax.shard_map(shards, mesh=mesh, in_specs=in_specs, out_specs=out_specs, check_vma=False)
```

profile of v0, /device:TPU:1, one launch (start us, length us, event | category | flops | bytes accessed | tf_op | source)
XLA Modules:
  0.0 692.3 jit_solution(16728772796914390734)
XLA Ops:
  6.5 1.0 copy.75
  7.5 9.3 %all_gather.6 = bf16[8,8,2,1024]{3,1,2,0:T(8,128)(2,1)} all-gather(bf16[2,8,2,1024]{3,1,2,0:T(8,128)(2,1)S(1)} %copy.75), channel_id=1, replica_groups=mesh['grp'=4,'tp'=64] {'grp'}, dimensions={0}, use_global_device_ids=true | all-gather | bytes 327680 | tf_op jit(solution)/shard_map/all_gather | solution.py:98
  16.9 0.0 all-gather.2.cloned.1.call-update
  16.9 0.0 copy-start.7
  16.9 0.8 convert_element_type.73
  17.7 1.1 fusion.31
  18.8 1.4 fusion.23
  20.3 0.5 fusion.24
  20.8 0.1 pad_maximum_fusion
  20.9 2.6 collective-permute-start
  23.5 8.4 %collective-permute-start.1 = (bf16[128,2,1024]{2,0,1:T(8,128)(2,1)S(1)}, bf16[128,2,1024]{2,0,1:T(8,128)(2,1)}, u32[]{:S(2)}, u32[]{:S(2)}) collective-permute-start(bf16[128,2,1024]{2,0,1:T(8,128)(2,1)S(1)} %pad_maximum_fusion), channel_id=1, source_target_pairs={{0,3},{1,4},{2,5},{3,6},{4,7},{5,8},{6,9},{7,10},{8,11},{9,12},{10... | collective-permute-start | bytes 1572872 | tf_op jit(solution)/shard_map/ppermute | solution.py:14
  31.8 3.5 collective-permute-start.2
  35.3 4.5 collective-permute-start.3
  39.8 0.1 copy.70
  40.0 0.2 reduce-window.4
  40.1 0.1 reduce
  40.3 0.3 convert_reduce_fusion.4
  40.7 0.3 select_reduce_fusion
  41.1 0.2 compare_select_fusion
  41.3 0.1 fusion.34
  41.4 0.1 copy.88
  41.5 0.1 fusion.37
  41.6 2.1 convolution_convert_fusion.1
  43.7 0.1 compare_and_fusion
  43.9 0.4 convolution_bitcast_fusion
  44.4 0.1 compare_and_fusion.1
  44.5 0.2 copy.73
  44.7 269.5 %gather_fusion = f32[81920,16]{1,0:T(8,128)} fusion(f32[16,1024]{0,1:T(8,128)S(1)} %copy.73, s32[81920]{0:T(1024)S(1)} %broadcast_clamp_fusion), kind=kCustom, calls=%fused_computation | custom fusion | bytes 10813440 | tf_op jit(solution)/shard_map/gather | solution.py:88
  314.1 23.4 %copy.85 = f32[128,640,16]{1,0,2:T(8,128)} copy(f32[128,640,16]{2,1,0:T(8,128)} %bitcast.80) | data formatting | bytes 10485760 | tf_op jit(solution)/shard_map/gather | solution.py:88
  337.5 0.2 copy.71
  337.7 215.5 %gather_fusion.1 = f32[65536,16]{1,0:T(8,128)} fusion(f32[16,1024]{0,1:T(8,128)S(1)} %copy.73, s32[65536]{0:T(1024)S(1)} %broadcast_clamp_fusion.1), kind=kCustom, calls=%fused_computation.1 | custom fusion | bytes 8650752 | tf_op jit(solution)/shard_map/gather | solution.py:112
  553.2 20.9 %copy.78 = f32[128,512,16]{1,0,2:T(8,128)} copy(f32[128,512,16]{2,1,0:T(8,128)} %bitcast.81) | data formatting | bytes 8388608 | tf_op jit(solution)/shard_map/gather | solution.py:112
  574.1 0.2 mul.95
  574.3 0.7 copy.89
  575.1 1.1 constant_dynamic-update-slice_fusion.4
  576.2 1.1 constant_dynamic-update-slice_fusion.3
  577.3 1.1 constant_dynamic-update-slice_fusion.2
  578.3 1.1 constant_dynamic-update-slice_fusion.1
  579.5 0.2 fusion.49
  579.7 1.5 copy.72
  581.2 0.7 copy.69
  581.9 4.0 fusion.50
  585.9 2.3 copy-done.2
  588.2 1.3 fusion.1
  589.5 0.0 all-gather.2.cloned.1.call-done
  589.5 11.3 %fusion.47 = (bf16[8,512,2,512]{3,1,2,0:T(8,128)(2,1)}, bf16[8,512,2,512]{3,1,2,0:T(8,128)(2,1)}) fusion(bf16[8,512,2,1024]{3,1,2,0:T(8,128)(2,1)} %all-gather.2.cloned.1.call-done), kind=kLoop, calls=%fused_computation.109 | loop fusion | bytes 33554432 | tf_op jit(solution)/shard_map/jit(_take)/gather | solution.py:99
  600.9 4.1 gather_fusion.2
  604.9 5.5 gather_fusion.3
  610.4 2.6 maximum_select_fusion
  613.0 2.5 fusion.48
  615.5 4.8 copy.76
  620.3 2.8 reshape_squeeze.14
  623.1 6.2 fusion.51
  629.3 11.7 %reshape.295 = f32[16,128,2,512]{3,2,1,0:T(2,128)} reshape(f32[16,128,1024]{2,1,0:T(8,128)} %fusion.51) | data formatting | bytes 16777216 | tf_op jit(solution)/shard_map/reshape | solution.py:110
  641.0 14.2 %multiply_reduce_fusion = f32[16,128,512]{2,1,0:T(8,128)S(1)} fusion(f32[16,128,2,512]{3,2,1,0:T(2,128)} %reshape.295, f32[128,2]{1,0:T(8,128)S(1)} %get-tuple-element.33), kind=kLoop, calls=%fused_computation.4 | loop fusion | flops 3145728 | bytes 12583936 | tf_op jit(solution)/shard_map/reduce_sum | solution.py:111
  655.2 0.4 fusion.44
  655.6 1.4 fusion.5
  657.1 3.6 mul.93
  660.7 7.7 %mul.94 = bf16[16,128,1024]{2,1,0:T(8,128)(2,1)} reshape(bf16[16,128,2,512]{3,2,1,0:T(2,128)(2,1)} %mul.93) | data formatting | bytes 8388608 | tf_op jit(solution)/shard_map/mul | solution.py:118
  668.4 4.8 copy.81
  673.2 2.7 reshape_squeeze.15
  676.0 4.4 fusion.14
  680.4 3.9 fusion.28
  684.3 1.2 convolution_convert_fusion
  (54 shorter events, 0.3 us)
Async XLA Ops:
  6.5 12.3 %copy-start = (bf16[1024,1024]{1,0:T(8,128)(2,1)S(1)}, bf16[1024,1024]{1,0:T(8,128)(2,1)}, u32[]{:S(2)}) copy-start(bf16[1024,1024]{1,0:T(8,128)(2,1)} %param.15) | copy-start | bytes 6291460
  6.5 13.8 %copy-start.4 = (bf16[128,1024]{1,0:T(8,128)(2,1)S(1)}, bf16[128,1024]{1,0:T(8,128)(2,1)}, u32[]{:S(2)}) copy-start(bf16[128,1024]{1,0:T(8,128)(2,1)} %param.12) | copy-start | bytes 786436
  6.5 583.0 %all-gather.2.cloned.1.call-start = ((), (), s32[]{:S(2)}) async-start(), calls=%async_computation | async-start | bytes 17039360 | tf_op jit(solution)/shard_map/all_gather | solution.py:99
  16.9 3.4 copy-start.7
  18.8 21.0 %copy-start.8 = (s32[1,128]{1,0:T(1,128)S(1)}, s32[1,128]{1,0:T(1,128)}, u32[]{:S(2)}) copy-start(s32[1,128]{1,0:T(1,128)} %param.22) | copy-start | bytes 1540
  20.3 20.3 %copy-start.10 = (s32[1,128]{1,0:T(1,128)S(1)}, s32[1,128]{1,0:T(1,128)}, u32[]{:S(2)}) copy-start(s32[1,128]{1,0:T(1,128)} %param.23) | copy-start | bytes 1540
  20.9 554.2 %collective-permute-start = (bf16[128,2,1024]{2,0,1:T(8,128)(2,1)S(1)}, bf16[128,2,1024]{2,0,1:T(8,128)(2,1)}, u32[]{:S(2)}, u32[]{:S(2)}) collective-permute-start(bf16[128,2,1024]{2,0,1:T(8,128)(2,1)S(1)} %pad_maximum_fusion), channel_id=1, source_target_pairs={{0,4},{1,5},{2,6},{3,7},{4,8},{5,9},{6,10},{7,11},{8,12},{9,13},{1... | collective-permute-start | bytes 1572872 | tf_op jit(solution)/shard_map/ppermute | solution.py:14
  23.5 552.7 %collective-permute-start.1 = (bf16[128,2,1024]{2,0,1:T(8,128)(2,1)S(1)}, bf16[128,2,1024]{2,0,1:T(8,128)(2,1)}, u32[]{:S(2)}, u32[]{:S(2)}) collective-permute-start(bf16[128,2,1024]{2,0,1:T(8,128)(2,1)S(1)} %pad_maximum_fusion), channel_id=1, source_target_pairs={{0,3},{1,4},{2,5},{3,6},{4,7},{5,8},{6,9},{7,10},{8,11},{9,12},{10... | collective-permute-start | bytes 1572872 | tf_op jit(solution)/shard_map/ppermute | solution.py:14
  31.8 545.4 %collective-permute-start.2 = (bf16[128,2,1024]{2,0,1:T(8,128)(2,1)S(1)}, bf16[128,2,1024]{2,0,1:T(8,128)(2,1)}, u32[]{:S(2)}, u32[]{:S(2)}) collective-permute-start(bf16[128,2,1024]{2,0,1:T(8,128)(2,1)S(1)} %pad_maximum_fusion), channel_id=1, source_target_pairs={{0,2},{1,3},{2,4},{3,5},{4,6},{5,7},{6,8},{7,9},{8,10},{9,11},{10,... | collective-permute-start | bytes 1572872 | tf_op jit(solution)/shard_map/ppermute | solution.py:14
  35.3 543.0 %collective-permute-start.3 = (bf16[128,2,1024]{2,0,1:T(8,128)(2,1)S(1)}, bf16[128,2,1024]{2,0,1:T(8,128)(2,1)}, u32[]{:S(2)}, u32[]{:S(2)}) collective-permute-start(bf16[128,2,1024]{2,0,1:T(8,128)(2,1)S(1)} %pad_maximum_fusion), channel_id=1, source_target_pairs={{0,1},{1,2},{2,3},{3,4},{4,5},{5,6},{6,7},{7,8},{8,9},{9,10},{10,1... | collective-permute-start | bytes 1572872 | tf_op jit(solution)/shard_map/ppermute | solution.py:14
  41.2 2.7 copy-start.11
  41.2 2.7 copy-start.12
  41.3 3.1 copy-start.9
  337.7 244.2 %copy-start.5 = (bf16[128,1024]{0,1:T(8,128)(2,1)}, bf16[128,1024]{0,1:T(8,128)(2,1)S(1)}, u32[]{:S(2)}) copy-start(bf16[128,1024]{0,1:T(8,128)(2,1)S(1)} %copy.71) | copy-start | bytes 786436
  585.9 2.3 copy-start.2
  641.0 14.2 %copy-start.3 = (f32[128,512,16]{1,0,2:T(8,128)S(1)}, f32[128,512,16]{1,0,2:T(8,128)}, u32[]{:S(2)}) copy-start(f32[128,512,16]{1,0,2:T(8,128)} %copy.78) | copy-start | bytes 12582916
  680.4 3.9 copy-start.6
  680.4 5.1 copy-start.1
Sparse Core Ops, SparseCore 0:
  17.0 206.5 all-gather.1
where the time goes:
time: 694 us; the launch traced here: 692 us
  local copies, waits for them, and re-layouts  602 us (87%)
  matrix products  24.1 us (3%)
  other arithmetic  23.5 us (3%)
  starting transfers between devices  19 us (3%)
  between operations  13.9 us (2%)
  blocking collectives  9.31 us (1%)
    gather x2, local copies, waits for them, and re-layouts, shards(): scores = scores + table_heads[:, dist]  293 us
    gather x2, local copies, waits for them, and re-layouts, shards(): fresh = fresh + table_heads[:, dist_pre]  236 us
    gather x3, local copies, waits for them, and re-layouts, shards(): jnp.take(lax.all_gather(owners, 'tp', axis=1, tiled=True), row_slots, axi...  20.8 us
    ppermute x4, starting transfers between devices, shifted(): return lax.ppermute(array, axis, pairs)  19 us
    reduce_sum x1, other arithmetic, shards(): fresh = jnp.sum(s_all * slot_pick[None, :, :, None], axis=2)  14.2 us
  transfers between devices with their start and end apart: 5, of which 0 were waited for; matrix products, arithmetic and copies ran while one was open for 80% of the time, Pallas kernels for 0%

commit v1 on v0

v1 whole, which is shorter than its diff:
```python
import jax
import jax.numpy as jnp
from jax import lax
from jax.experimental import pallas as pl
from jax.experimental.pallas import tpu as pltpu
from jax.sharding import PartitionSpec as P

D = 1024
H = 16
TOK = 128
LMAX = 512
KEYS = LMAX + TOK
PREFIX = 512
SPAN = 1024
NEG = -1e30


def attend_kernel(
    pos_ref,
    hid_ref,
    gain_ref,
    wq_ref,
    wk_ref,
    wv_ref,
    wo_ref,
    rt_ref,
    grp_ref,
    pk_ref,
    pv_ref,
    out_ref,
    n_ref,
    q_ref,
    k_ref,
    v_ref,
    b_ref,
    mix_ref,
):
    f32 = jnp.float32
    bf16 = jnp.bfloat16
    gain = gain_ref[...].astype(f32)

    def norm(i, _):
        rows = pl.ds(pl.multiple_of(i * TOK, TOK), TOK)
        x = hid_ref[rows, :].astype(f32)
        ms = jnp.mean(x * x, axis=1, keepdims=True)
        n_ref[rows, :] = (x * lax.rsqrt(ms + 1e-06) * gain).astype(bf16)
        return 0

    lax.fori_loop(0, KEYS // TOK, norm, 0)

    def project(i, _):
        cols = pl.ds(pl.multiple_of(i * 256, 256), 256)
        q_ref[:, cols] = jnp.dot(
            n_ref[pl.ds(LMAX, TOK), :], wq_ref[:, cols], preferred_element_type=f32
        ).astype(bf16)
        k_ref[:, cols] = jnp.dot(n_ref[...], wk_ref[:, cols], preferred_element_type=f32).astype(
            bf16
        )
        v_ref[:, cols] = jnp.dot(n_ref[...], wv_ref[:, cols], preferred_element_type=f32).astype(
            bf16
        )
        return 0

    lax.fori_loop(0, D // 256, project, 0)

    lane = lax.broadcasted_iota(jnp.int32, (H, 128), 1)

    def bias(a, _):
        pos = pos_ref[a]
        rows = pl.ds(pl.multiple_of(a * H, H), H)
        off = PREFIX - 1 - pos
        base = lax.shift_right_logical(off, 7)
        keep = 128 - jnp.bitwise_and(off, 127)
        turn = jnp.bitwise_and(keep, 127)
        tiles = [
            pltpu.roll(rt_ref[:, pl.ds(pl.multiple_of((base + j) * 128, 128), 128)], turn, 1)
            for j in range(5)
        ]
        for j in range(4):
            b_ref[5 + j, rows, :] = jnp.where(
                lane < keep, tiles[j], tiles[j + 1]
            )
        turn = jnp.bitwise_and(a + 1, 127)
        tiles = [pltpu.roll(rt_ref[:, 384 + 128 * j : 512 + 128 * j], turn, 1) for j in range(6)]
        low = LMAX + a - pos
        for j in range(5):
            col = lane + 128 * j
            good = (col >= low) & (col <= LMAX + a)
            b_ref[j, rows, :] = jnp.where(
                good, jnp.where(lane < a + 1, tiles[j], tiles[j + 1]), NEG
            )
        return 0

    lax.fori_loop(0, TOK, bias, 0)

    first = grp_ref[...] == 0
    first2 = jnp.concatenate([first, first], axis=0)
    half = lax.broadcasted_iota(jnp.int32, (TOK, 128), 1) < 64
    nt = (((1,), (1,)), ((), ()))

    def heads(p, _):
        cols = pl.ds(pl.multiple_of(p * 128, 128), 128)
        q = q_ref[:, cols].astype(f32)
        qq = jnp.concatenate([jnp.where(half, q, 0.0), jnp.where(half, 0.0, q)], axis=0)
        qg = jnp.concatenate(
            [jnp.where(first2, qq, 0.0), jnp.where(first2, 0.0, qq)], axis=1
        ).astype(bf16)
        kcat = jnp.concatenate(
            [pk_ref[:, s, :, cols].reshape(PREFIX, 128) for s in range(2)], axis=1
        )
        vcat = jnp.concatenate(
            [pv_ref[:, s, :, cols].reshape(PREFIX, 128) for s in range(2)], axis=1
        )
        bias2 = jnp.concatenate(
            [
                jnp.concatenate(
                    [b_ref[j, pl.ds(2 * p + e, TOK, stride=H), :] for j in range(9)], axis=1
                )
                for e in range(2)
            ],
            axis=0,
        )
        suf = (
            lax.dot_general(qq.astype(bf16), k_ref[:, cols], nt, preferred_element_type=f32)
            + bias2[:, :KEYS]
        )
        pre = lax.dot_general(qg, kcat, nt, preferred_element_type=f32) + bias2[:, KEYS:]
        top = jnp.maximum(
            jnp.max(suf, axis=1, keepdims=True), jnp.max(pre, axis=1, keepdims=True)
        )
        esuf = jnp.exp(suf - top)
        epre = jnp.exp(pre - top)
        total = jnp.sum(esuf, axis=1, keepdims=True) + jnp.sum(epre, axis=1, keepdims=True)
        osuf = jnp.dot(esuf.astype(bf16), v_ref[:, cols], preferred_element_type=f32)
        opre = jnp.dot(epre.astype(bf16), vcat, preferred_element_type=f32)
        o = (osuf + jnp.where(first2, opre[:, :128], opre[:, 128:])) / total
        mix_ref[:, cols] = jnp.where(half, o[:TOK], o[TOK:]).astype(bf16)
        return 0

    lax.fori_loop(0, H // 2, heads, 0)

    out_ref[...] = jnp.dot(mix_ref[...], wo_ref[...], preferred_element_type=f32).astype(bf16)


def attend(pos, hid, gain, wq, wk, wv, wo, rt, grp, pk, pv):
    vmem = pl.BlockSpec(memory_space=pltpu.VMEM)
    return pl.pallas_call(
        attend_kernel,
        out_shape=jax.ShapeDtypeStruct((TOK, D), jnp.bfloat16),
        in_specs=[pl.BlockSpec(memory_space=pltpu.SMEM)] + [vmem] * 10,
        out_specs=vmem,
        scratch_shapes=[
            pltpu.VMEM((KEYS, D), jnp.bfloat16),
            pltpu.VMEM((TOK, D), jnp.bfloat16),
            pltpu.VMEM((KEYS, D), jnp.bfloat16),
            pltpu.VMEM((KEYS, D), jnp.bfloat16),
            pltpu.VMEM(((KEYS + PREFIX) // 128, TOK * H, 128), jnp.float32),
            pltpu.VMEM((TOK, D), jnp.bfloat16),
        ],
        compiler_params=pltpu.CompilerParams(vmem_limit_bytes=56 << 20),
        name="attend",
    )(pos, hid, gain, wq, wk, wv, wo, rt, grp, pk, pv)


def shifted(array, axis, by):
    peers = lax.axis_size(axis)
    pairs = [(i, i + by) for i in range(peers) if 0 <= i + by < peers]
    return lax.ppermute(array, axis, pairs)


def shards(
    hidden,
    ln_gain,
    w_query,
    w_key,
    w_value,
    w_out,
    rel_bias,
    prefix_cache,
    bucket_of_distance,
    slot_of_group,
    suffix_lengths,
    request_group,
):
    tp_index = lax.axis_index("tp")
    row_index = lax.axis_index("grp")
    earlier = [shifted(hidden, "tp", step) for step in range(LMAX // TOK, 0, -1)]
    hid = jnp.concatenate(earlier + [hidden], axis=0)

    row_slots = lax.dynamic_slice_in_dim(slot_of_group, row_index * 2, 2)
    owners = lax.all_gather(prefix_cache, "grp", axis=0, tiled=True)
    mine = jnp.take(owners, row_slots, axis=0)
    kv = lax.all_gather(mine, "tp", axis=1, tiled=True)
    kv = kv.reshape(2, 16, 32, 2, D)
    pk = kv[:, :, :, 0].transpose(1, 0, 2, 3)
    pv = kv[:, :, :, 1].transpose(1, 0, 2, 3)

    lens = suffix_lengths[0]
    ends = jnp.cumsum(lens)
    starts = ends - lens
    rows = tp_index * TOK + jnp.arange(TOK)
    req = jnp.minimum(jnp.sum((rows[:, None] >= ends[None, :]).astype(jnp.int32), axis=1), 127)
    onehot = req[:, None] == jnp.arange(lens.shape[0])[None, :]
    pos = rows - jnp.sum(jnp.where(onehot, starts[None, :], 0), axis=1)
    grp = jnp.sum(jnp.where(onehot, request_group[0][None, :], 0), axis=1)

    table = jnp.dot(
        rel_bias.T,
        jax.nn.one_hot(bucket_of_distance[::-1], rel_bias.shape[0], dtype=jnp.float32, axis=0),
        precision=lax.Precision.HIGHEST,
    )
    rt = jnp.pad(table, ((0, 0), (0, 128)))
    return attend(
        pos, hid, ln_gain[None, :], w_query, w_key, w_value, w_out, rt, grp[:, None], pk, pv
    )


def solution(mesh):
    in_specs = (
        P(("grp", "tp"), None),
        P(),
        P(),
        P(),
        P(),
        P(),
        P(),
        P("grp", "tp", None, None),
        P(),
        P(),
        P("grp", None),
        P("grp", None),
    )
    out_specs = P(("grp", "tp"), None)
    return jax.shard_map(shards, mesh=mesh, in_specs=in_specs, out_specs=out_specs, check_vma=False)
```

time: 694 us -> 166 us (0.24)
  local copies, waits for them, and re-layouts: 602 us -> 10.8 us
  waiting for transfers between devices: 0.05 us -> 77.4 us
  Pallas kernels: 0 us -> 33.1 us
  matrix products: 24.1 us -> 0.17 us
  other arithmetic: 23.5 us -> 4.03 us
    gather x7 -> x1, local copies, waits for them, and re-layouts: 550 us -> 0.55 us  [shards(): mine = jnp.take(owners, row_slots, axis=0)]
    all_gather x1, waiting for transfers between devices: 0.02 us -> 66.6 us  [shards(): kv = lax.all_gather(mine, 'tp', axis=1, tiled=True)]
    pallas_call x0 -> x1, Pallas kernels: none -> 33.1 us  [attend(): pl.pallas_call(attend_kernel, out_shape=jax.ShapeDtypeStruct((TOK, D), jn...]
    dot_general x9 -> x1, matrix products: 24.1 us -> 0.17 us  [shards(): jnp.dot(rel_bias.T, jax.nn.one_hot(bucket_of_distance[::-1], rel_bias.sha...]
    reduce_sum x6 -> x2, other arithmetic: 18.5 us -> 1 us  [the longest x1 0.83 us: shards(): grp = jnp.sum(jnp.where(onehot, request_group[0][None, :], 0), axis=1)]
    slice x6 -> x1, local copies, waits for them, and re-layouts: 14.5 us -> 2.66 us  [shards(): pv = kv[:, :, :, 1].transpose(1, 0, 2, 3)]
    mul x3 -> x0, local copies, waits for them, and re-layouts: 11.5 us -> none  [shards(): rounded[:, :, None, :] * slot_pick.astype(jnp.bfloat16)[None, :, :, None]]
    reshape x2 -> x1, local copies, waits for them, and re-layouts: 11.9 us -> 0.76 us  [the longest x1 11.7 us: shards(): s_all = s_all.reshape(heads, tok, slots_here, count)]
  transfers between devices with their start and end apart: 5 -> 5, of which waited for: 0 -> 3; matrix products, arithmetic and copies ran while one was open for 80% -> 4% of each run, Pallas kernels for 0% -> 0%
where the time goes in v1:
time: 166 us; the launch traced here: 165 us
  waiting for transfers between devices  77.4 us (47%)
  Pallas kernels  33.1 us (20%)
  starting transfers between devices  17.3 us (10%)
  between operations  13.5 us (8%)
  local copies, waits for them, and re-layouts  10.8 us (7%)
  blocking collectives  8.86 us (5%)
  other arithmetic  4.03 us (2%)
    all_gather x1, waiting for transfers between devices, shards(): kv = lax.all_gather(mine, 'tp', axis=1, tiled=True)  66.6 us
    pallas_call x1, Pallas kernels, attend(): pl.pallas_call(attend_kernel, out_shape=jax.ShapeDtypeStruct((TOK, D), jn...  33.1 us
    ppermute x4, starting transfers between devices, shifted(): return lax.ppermute(array, axis, pairs)  17.3 us
    ppermute x4, waiting for transfers between devices, shifted(): return lax.ppermute(array, axis, pairs)  10.8 us
    all_gather x1, blocking collectives, shards(): owners = lax.all_gather(prefix_cache, 'grp', axis=0, tiled=True)  8.86 us
  transfers between devices with their start and end apart: 5, of which 3 were waited for; matrix products, arithmetic and copies ran while one was open for 4% of the time, Pallas kernels for 0%

profile of v1, /device:TPU:1, one launch (start us, length us, event | category | flops | bytes accessed | tf_op | source)
XLA Modules:
  0.0 165.2 jit_solution(15058270690234443110)
XLA Ops:
  6.5 0.0 copy-start
  6.5 0.0 copy-start.2
  6.5 0.0 all-gather.2.cloned.1.call-start
  6.5 0.8 compare_and_fusion
  7.3 0.9 copy.30
  8.2 8.9 %all_gather.6 = bf16[8,8,2,1024]{3,1,2,0:T(8,128)(2,1)S(1)} all-gather(bf16[2,8,2,1024]{3,1,2,0:T(8,128)(2,1)S(1)} %copy.30), channel_id=1, replica_groups=mesh['grp'=4,'tp'=64] {'grp'}, dimensions={0}, use_global_device_ids=true | all-gather | bytes 327680 | tf_op jit(solution)/shard_map/all_gather | solution.py:191
  17.0 0.5 gather_fusion
  17.6 0.7 broadcast_select_fusion
  18.3 0.0 all-gather.2.cloned.1.call-update
  18.3 1.8 %collective-permute-start = (bf16[128,1024]{1,0:T(8,128)(2,1)}, bf16[128,1024]{1,0:T(8,128)(2,1)S(1)}, u32[]{:S(2)}, u32[]{:S(2)}) collective-permute-start(bf16[128,1024]{1,0:T(8,128)(2,1)} %param.12), channel_id=1, source_target_pairs={{0,4},{1,5},{2,6},{3,7},{4,8},{5,9},{6,10},{7,11},{8,12},{9,13},{1... | collective-permute-start | bytes 786440 | tf_op jit(solution)/shard_map/ppermute | solution.py:168
  20.1 7.6 %collective-permute-start.1 = (bf16[128,1024]{1,0:T(8,128)(2,1)}, bf16[128,1024]{1,0:T(8,128)(2,1)S(1)}, u32[]{:S(2)}, u32[]{:S(2)}) collective-permute-start(bf16[128,1024]{1,0:T(8,128)(2,1)} %param.12), channel_id=1, source_target_pairs={{0,3},{1,4},{2,5},{3,6},{4,7},{5,8},{6,9},{7,10},{8,11},{9,12},{10... | collective-permute-start | bytes 786440 | tf_op jit(solution)/shard_map/ppermute | solution.py:168
  27.7 3.5 %collective-permute-start.2 = (bf16[128,1024]{1,0:T(8,128)(2,1)}, bf16[128,1024]{1,0:T(8,128)(2,1)S(1)}, u32[]{:S(2)}, u32[]{:S(2)}) collective-permute-start(bf16[128,1024]{1,0:T(8,128)(2,1)} %param.12), channel_id=1, source_target_pairs={{0,2},{1,3},{2,4},{3,5},{4,6},{5,7},{6,8},{7,9},{8,10},{9,11},{10,... | collective-permute-start | bytes 786440 | tf_op jit(solution)/shard_map/ppermute | solution.py:168
  31.2 4.5 %collective-permute-start.3 = (bf16[128,1024]{1,0:T(8,128)(2,1)}, bf16[128,1024]{1,0:T(8,128)(2,1)S(1)}, u32[]{:S(2)}, u32[]{:S(2)}) collective-permute-start(bf16[128,1024]{1,0:T(8,128)(2,1)} %param.12), channel_id=1, source_target_pairs={{0,1},{1,2},{2,3},{3,4},{4,5},{5,6},{6,7},{7,8},{8,9},{9,10},{10,1... | collective-permute-start | bytes 786440 | tf_op jit(solution)/shard_map/ppermute | solution.py:168
  35.7 0.8 copy.29
  36.5 0.2 reduce-window.4
  36.6 0.1 reduce
  36.8 0.8 rev.3
  37.5 0.2 convert_reduce_fusion
  37.7 0.7 fusion.1
  38.4 0.0 copy-done
  38.4 0.2 convolution_bitcast_fusion
  38.6 0.8 select_reduce_fusion
  39.4 0.6 fusion.2.pos_ref
  40.0 0.8 copy.33.grp_ref
  40.7 1.3 broadcast_in_dim.50.gain_ref
  42.0 0.6 pad.4.rt_ref
  42.7 0.0 collective-permute-done
  42.7 0.0 collective-permute-done.1
  42.7 3.0 %collective-permute-done.2 = bf16[128,1024]{1,0:T(8,128)(2,1)S(1)} collective-permute-done((bf16[128,1024]{1,0:T(8,128)(2,1)}, bf16[128,1024]{1,0:T(8,128)(2,1)S(1)}, u32[]{:S(2)}, u32[]{:S(2)}) %collective-permute-start.2) | collective-permute-done | bytes 262176 | tf_op jit(solution)/shard_map/ppermute | solution.py:168
  45.7 7.8 %collective-permute-done.3 = bf16[128,1024]{1,0:T(8,128)(2,1)S(1)} collective-permute-done((bf16[128,1024]{1,0:T(8,128)(2,1)}, bf16[128,1024]{1,0:T(8,128)(2,1)S(1)}, u32[]{:S(2)}, u32[]{:S(2)}) %collective-permute-start.3) | collective-permute-done | bytes 262176 | tf_op jit(solution)/shard_map/ppermute | solution.py:168
  53.6 0.0 copy-done.2
  53.6 0.0 copy-start.1
  53.6 66.6 %all-gather.2.cloned.1.call-done = bf16[2,512,2,1024]{3,1,2,0:T(8,128)(2,1)} async-done(((bf16[2,8,2,1024]{3,1,2,0:T(8,128)(2,1)}), bf16[2,512,2,1024]{3,1,2,0:T(8,128)(2,1)}) %all-gather.2.cloned.1.call-update) | async-done | bytes 4194320 | tf_op jit(solution)/shard_map/all_gather | solution.py:193
  120.2 2.7 %fusion.3 = (bf16[2,16,32,1,1024]{4,2,1,3,0:T(8,128)(2,1)S(1)}, bf16[2,16,32,1,1024]{4,2,1,3,0:T(8,128)(2,1)S(1)}) fusion(bf16[2,16,32,2,1024]{4,2,1,3,0:T(8,128)(2,1)} %bitcast.21), kind=kLoop, calls=%fused_computation.24 | loop fusion | bytes 8388608 | tf_op jit(solution)/shard_map/slice | solution.py:196
  122.9 0.0 copy-done.1
  122.9 2.4 %copy_bitcast_fusion = (bf16[16,2,32,1024]{3,2,1,0:T(8,128)(2,1)}, bf16[16,2,32,1024]{3,2,1,0:T(8,128)(2,1)}) fusion(bf16[2,16,32,1,1024]{4,2,1,3,0:T(8,128)(2,1)S(1)} %get-tuple-element.9, bf16[2,16,32,1,1024]{4,2,1,3,0:T(8,128)(2,1)S(1)} %get-tuple-element.10), kind=kLoop, calls=%fused_computation.1 | loop fusion | bytes 8388608 | tf_op jit(solution)/shard_map/transpose | solution.py:196
  125.3 33.1 %attend.1 = bf16[128,1024]{1,0:T(8,128)(2,1)} custom-call(s32[128]{0:T(128)} %fusion.2.pos_ref, bf16[640,1024]{1,0:T(8,128)(2,1)} %copy-done.1, bf16[1,1024]{1,0:T(2,128)(2,1)} %broadcast_in_dim.50.gain_ref, bf16[1024,1024]{1,0:T(8,128)(2,1)} %wq_ref.1, bf16[1024,1024]{1,0:T(8,128)(2,1)} %wk_ref.1, bf16[1024,1024]{1,0:T(8,128)(2,1)} %wv_ref.1, ...), custom_call_target="tpu_custom_call" | custom-call | tf_op jit(solution)/shard_map/attend/pallas_call | solution.py:147
  (8 shorter events, 0.1 us)
Async XLA Ops:
  6.5 31.8 %copy-start = (f32[32,16]{0,1:T(8,128)S(1)}, f32[32,16]{0,1:T(8,128)}, u32[]{:S(2)}) copy-start(f32[32,16]{0,1:T(8,128)} %param.18) | copy-start | bytes 6148
  6.5 47.0 %copy-start.2 = (bf16[128,1024]{1,0:T(8,128)(2,1)S(1)}, bf16[128,1024]{1,0:T(8,128)(2,1)}, u32[]{:S(2)}) copy-start(bf16[128,1024]{1,0:T(8,128)(2,1)} %param.12) | copy-start | bytes 786436
  6.5 113.7 %all-gather.2.cloned.1.call-start = ((), (), s32[]{:S(2)}) async-start(), calls=%async_computation | async-start | bytes 4259840 | tf_op jit(solution)/shard_map/all_gather | solution.py:193
  18.3 24.3 %collective-permute-start = (bf16[128,1024]{1,0:T(8,128)(2,1)}, bf16[128,1024]{1,0:T(8,128)(2,1)S(1)}, u32[]{:S(2)}, u32[]{:S(2)}) collective-permute-start(bf16[128,1024]{1,0:T(8,128)(2,1)} %param.12), channel_id=1, source_target_pairs={{0,4},{1,5},{2,6},{3,7},{4,8},{5,9},{6,10},{7,11},{8,12},{9,13},{1... | collective-permute-start | bytes 786440 | tf_op jit(solution)/shard_map/ppermute | solution.py:168
  20.1 22.6 %collective-permute-start.1 = (bf16[128,1024]{1,0:T(8,128)(2,1)}, bf16[128,1024]{1,0:T(8,128)(2,1)S(1)}, u32[]{:S(2)}, u32[]{:S(2)}) collective-permute-start(bf16[128,1024]{1,0:T(8,128)(2,1)} %param.12), channel_id=1, source_target_pairs={{0,3},{1,4},{2,5},{3,6},{4,7},{5,8},{6,9},{7,10},{8,11},{9,12},{10... | collective-permute-start | bytes 786440 | tf_op jit(solution)/shard_map/ppermute | solution.py:168
  27.7 18.0 %collective-permute-start.2 = (bf16[128,1024]{1,0:T(8,128)(2,1)}, bf16[128,1024]{1,0:T(8,128)(2,1)S(1)}, u32[]{:S(2)}, u32[]{:S(2)}) collective-permute-start(bf16[128,1024]{1,0:T(8,128)(2,1)} %param.12), channel_id=1, source_target_pairs={{0,2},{1,3},{2,4},{3,5},{4,6},{5,7},{6,8},{7,9},{8,10},{9,11},{10,... | collective-permute-start | bytes 786440 | tf_op jit(solution)/shard_map/ppermute | solution.py:168
  31.2 22.3 %collective-permute-start.3 = (bf16[128,1024]{1,0:T(8,128)(2,1)}, bf16[128,1024]{1,0:T(8,128)(2,1)S(1)}, u32[]{:S(2)}, u32[]{:S(2)}) collective-permute-start(bf16[128,1024]{1,0:T(8,128)(2,1)} %param.12), channel_id=1, source_target_pairs={{0,1},{1,2},{2,3},{3,4},{4,5},{5,6},{6,7},{7,8},{8,9},{9,10},{10,1... | collective-permute-start | bytes 786440 | tf_op jit(solution)/shard_map/ppermute | solution.py:168
  53.6 69.3 %copy-start.1 = (bf16[640,1024]{1,0:T(8,128)(2,1)}, bf16[640,1024]{1,0:T(8,128)(2,1)S(1)}, u32[]{:S(2)}) copy-start(bf16[640,1024]{1,0:T(8,128)(2,1)S(1)} %constant_dynamic-update-slice_fusion.hid_ref) | copy-start | bytes 3932164
Sparse Core Ops, SparseCore 0:
  18.5 101.7 all-gather.1

commit v2 on v1

v2 whole, which is shorter than its diff:
```python
import jax
import jax.numpy as jnp
from jax import lax
from jax.experimental import pallas as pl
from jax.experimental.pallas import tpu as pltpu
from jax.sharding import PartitionSpec as P

D = 1024
H = 16
TOK = 128
LMAX = 512
KEYS = LMAX + TOK
PREFIX = 512
SPAN = 1024
NEG = -1e30
MESH = pl.DeviceIdType.MESH


def layer_kernel(
    pos_ref,
    slot_ref,
    hid_ref,
    pre_ref,
    gain_ref,
    rt_ref,
    grp_ref,
    place_ref,
    wq_hbm,
    wk_hbm,
    wv_hbm,
    wo_hbm,
    out_ref,
    wq_ref,
    wk_ref,
    wv_ref,
    wo_ref,
    own_ref,
    z_ref,
    all_ref,
    pk_ref,
    pv_ref,
    n_ref,
    q_ref,
    k_ref,
    v_ref,
    s_ref,
    b_ref,
    mask_ref,
    mix_ref,
    send_sem,
    recv_sem,
    load_sem,
):
    f32 = jnp.float32
    bf16 = jnp.bfloat16
    g = lax.axis_index("grp")
    t = lax.axis_index("tp")
    y, x, z = t // 16, (t // 4) % 4, t % 4

    def tp_id(i):
        return (g, lax.rem(i + 128, 64))

    def z_id(d):
        return (g, y * 16 + x * 4 + lax.rem(z + d + 4, 4))

    def x_id(d):
        return (g, y * 16 + lax.rem(x + d + 4, 4) * 4 + z)

    def y_id(d):
        return (g, lax.rem(y + d + 4, 4) * 16 + x * 4 + z)

    used = []

    def copy(src, dst, device):
        i = len(used)
        out = pltpu.make_async_remote_copy(
            src_ref=src,
            dst_ref=dst,
            send_sem=send_sem.at[i],
            recv_sem=recv_sem.at[i],
            device_id=device,
            device_id_type=MESH,
        )
        out.start()
        used.append(out)
        return out

    loads = [
        pltpu.make_async_copy(src, dst, load_sem.at[i])
        for i, (src, dst) in enumerate(
            [(wq_hbm, wq_ref), (wk_hbm, wk_ref), (wv_hbm, wv_ref), (wo_hbm, wo_ref)]
        )
    ]
    for load in loads:
        load.start()

    row_ids = [(lax.rem(g + d, 4), t) for d in (1, 2, 3)]
    greet = row_ids + [tp_id(t + d) for d in (1, -1, 4, -4)]
    greet = greet + [ring(d) for ring in (x_id, y_id, z_id) for d in (1, -1)]
    barrier = pltpu.get_barrier_semaphore()
    for device in greet:
        pl.semaphore_signal(barrier, inc=1, device_id=device, device_id_type=MESH)
    pl.semaphore_wait(barrier, len(greet))

    own_ref[pl.ds(2 * g, 2)] = pre_ref[...]
    rows = [copy(pre_ref, own_ref.at[pl.ds(2 * g, 2)], device) for device in row_ids]
    block = [all_ref.at[pl.ds(TOK * i, TOK)] for i in range(4)]
    back4 = copy(hid_ref, block[0], tp_id(t + 4))
    for c in rows:
        c.wait_recv()
    for s in range(2):
        slot = jnp.full((8, 2 * D), slot_ref[2 * g + s], jnp.int32)
        chosen = own_ref[0].astype(f32)
        for i in range(1, 8):
            chosen = jnp.where(slot == i, own_ref[i].astype(f32), chosen)
        z_ref[z, s] = chosen.astype(bf16)

    def spread(buf, piece, me, ring):
        part = buf.at[piece(me)]
        return [copy(part, part, ring(1)), copy(part, part, ring(-1))]

    def onward(buf, piece, me, ring, first, step):
        first[0 if step == 1 else 1].wait_recv()
        part = buf.at[piece(lax.rem(me - step + 4, 4))]
        return copy(part, part, ring(step))

    zs = [spread(z_ref, lambda i, s=s: (i, s), z, z_id) for s in range(2)]
    back1 = copy(hid_ref, block[3], tp_id(t + 1))
    zfwd = [
        onward(z_ref, lambda i, s=s: (i, s), z, z_id, zs[s], 1 - 2 * s) for s in range(2)
    ]
    back4.wait_recv()
    back3 = copy(block[0], block[1], tp_id(t - 1))
    zs[0][1].wait_recv()
    zs[1][0].wait_recv()
    for c in zfwd:
        c.wait_recv()

    for s in range(2):
        for i in range(2):
            both = jnp.concatenate(
                [z_ref[2 * i, s].astype(f32), z_ref[2 * i + 1, s].astype(f32)], axis=0
            ).astype(bf16)
            pk_ref[y * 4 + x, s, 16 * i : 16 * (i + 1), :] = both[:, :D]
            pv_ref[y * 4 + x, s, 16 * i : 16 * (i + 1), :] = both[:, D:]

    def at_x(i, other, s):
        return (other * 4 + i, s)

    def at_y(i, other, s):
        return (i * 4 + other, s)

    lines = []
    for s in range(2):
        lines.append((pk_ref, s, x, y, x_id, y_id, at_x, at_y))
        lines.append((pv_ref, s, y, x, y_id, x_id, at_y, at_x))
    one = []
    for buf, s, me, other, ring, _, at, _ in lines:
        one.append(spread(buf, lambda i, s=s, at=at, o=other: at(i, o, s), me, ring))

    def second(line, shift):
        buf, s, me, other, _, ring, _, at = line
        chunk = lax.rem(me + shift + 4, 4)
        return spread(buf, lambda i: at(i, chunk, s), other, ring)

    def second_on(line, shift, first):
        buf, s, me, other, _, ring, _, at = line
        chunk = lax.rem(me + shift + 4, 4)
        step = 1 - 2 * s
        return onward(buf, lambda i: at(i, chunk, s), other, ring, first, step)

    two = [{0: second(line, 0)} for line in lines]
    far = []
    for line, first, rest in zip(lines, one, two):
        buf, s, me, other, ring, _, at, _ = line
        step = 1 - 2 * s
        far.append(onward(buf, lambda i: at(i, other, s), me, ring, first, step))
        rest[-step] = second(line, -step)
    for line, first, rest in zip(lines, one, two):
        step = 1 - 2 * line[1]
        first[1 if step == 1 else 0].wait_recv()
        rest[step] = second(line, step)

    back1.wait_recv()
    low = pl.ds(TOK * 2, TOK // 2)
    high = pl.ds(TOK * 2 + TOK // 2, TOK // 2)
    back2a = copy(all_ref.at[pl.ds(TOK * 3, TOK // 2)], all_ref.at[low], tp_id(t + 1))
    back3.wait_recv()
    back2b = copy(
        all_ref.at[pl.ds(TOK + TOK // 2, TOK // 2)], all_ref.at[high], tp_id(t - 1)
    )

    last = [second_on(line, 0, rest[0]) for line, rest in zip(lines, two)]
    for line, rest, c in zip(lines, two, far):
        c.wait_recv()
        rest[2] = second(line, 2)
    for shift in (1, -1, 2):
        last = last + [
            second_on(line, shift, rest[shift]) for line, rest in zip(lines, two)
        ]
    for line, rest in zip(lines, two):
        step = 1 - 2 * line[1]
        for shift in (0, 1, -1, 2):
            rest[shift][1 if step == 1 else 0].wait_recv()
    for c in last:
        c.wait_recv()
    back2a.wait_recv()
    back2b.wait_recv()
    for c in used:
        c.wait_send()

    all_ref[pl.ds(LMAX, TOK)] = hid_ref[...]
    for load in loads:
        load.wait()

    gain = gain_ref[...].astype(f32)

    def norm(i, _):
        rows = pl.ds(pl.multiple_of(i * TOK, TOK), TOK)
        x = all_ref[rows, :].astype(f32)
        ms = jnp.mean(x * x, axis=1, keepdims=True)
        n_ref[rows, :] = (x * lax.rsqrt(ms + 1e-06) * gain).astype(bf16)
        return 0

    lax.fori_loop(0, KEYS // TOK, norm, 0)

    def project(i, _):
        cols = pl.ds(pl.multiple_of(i * 256, 256), 256)
        q_ref[:, cols] = jnp.dot(
            n_ref[pl.ds(LMAX, TOK), :], wq_ref[:, cols], preferred_element_type=f32
        ).astype(bf16)
        k_ref[:, cols] = jnp.dot(n_ref[...], wk_ref[:, cols], preferred_element_type=f32).astype(
            bf16
        )
        v_ref[:, cols] = jnp.dot(n_ref[...], wv_ref[:, cols], preferred_element_type=f32).astype(
            bf16
        )
        return 0

    lax.fori_loop(0, D // 256, project, 0)

    lane = lax.broadcasted_iota(jnp.int32, (H, 128), 1)

    def slide(i, _):
        for a in [i * 4 + e for e in range(4)]:
            turn = jnp.bitwise_and(a + 1, 127)
            tiles = [pltpu.roll(rt_ref[:, 128 * j : 128 * (j + 1)], turn, 1) for j in range(9)]
            for j in range(8):
                s_ref[j, pl.ds(pl.multiple_of(a * H, H), H), :] = jnp.where(
                    lane < a + 1, tiles[j], tiles[j + 1]
                )
        return 0

    lax.fori_loop(0, TOK // 4, slide, 0)

    turned = s_ref.reshape(8, TOK, H, 128)
    wanted = b_ref.reshape(4, TOK, H, 128)

    def pick(i, _):
        for a in [i * 8 + e for e in range(8)]:
            for j in range(4):
                wanted[j, a] = turned[pos_ref[0, a] + j, pos_ref[1, a]]
        return 0

    lax.fori_loop(0, TOK // 8, pick, 0)

    row = lax.broadcasted_iota(jnp.int32, (TOK, KEYS), 0)
    col = lax.broadcasted_iota(jnp.int32, (TOK, KEYS), 1)
    mask_ref[...] = jnp.where(
        (col >= LMAX + row - place_ref[...]) & (col <= LMAX + row), 0.0, NEG
    )

    first = grp_ref[...] == 0
    first2 = jnp.concatenate([first, first], axis=0)
    half = lax.broadcasted_iota(jnp.int32, (TOK, 128), 1) < 64
    nt = (((1,), (1,)), ((), ()))

    def heads(p, _):
        cols = pl.ds(pl.multiple_of(p * 128, 128), 128)
        q = q_ref[:, cols].astype(f32)
        qq = jnp.concatenate([jnp.where(half, q, 0.0), jnp.where(half, 0.0, q)], axis=0)
        qg = jnp.concatenate(
            [jnp.where(first2, qq, 0.0), jnp.where(first2, 0.0, qq)], axis=1
        ).astype(bf16)
        kcat = jnp.concatenate(
            [pk_ref[:, s, :, cols].reshape(PREFIX, 128) for s in range(2)], axis=1
        )
        vcat = jnp.concatenate(
            [pv_ref[:, s, :, cols].reshape(PREFIX, 128) for s in range(2)], axis=1
        )
        def gather(ref, tiles):
            return jnp.concatenate(
                [
                    jnp.concatenate(
                        [ref[j, pl.ds(2 * p + e, TOK, stride=H), :] for j in tiles], axis=1
                    )
                    for e in range(2)
                ],
                axis=0,
            )

        mask = mask_ref[...]
        suf = (
            lax.dot_general(qq.astype(bf16), k_ref[:, cols], nt, preferred_element_type=f32)
            + gather(s_ref, range(3, 8))
            + jnp.concatenate([mask, mask], axis=0)
        )
        pre = lax.dot_general(qg, kcat, nt, preferred_element_type=f32) + gather(b_ref, range(4))
        top = jnp.maximum(
            jnp.max(suf, axis=1, keepdims=True), jnp.max(pre, axis=1, keepdims=True)
        )
        esuf = jnp.exp(suf - top)
        epre = jnp.exp(pre - top)
        total = jnp.sum(esuf, axis=1, keepdims=True) + jnp.sum(epre, axis=1, keepdims=True)
        osuf = jnp.dot(esuf.astype(bf16), v_ref[:, cols], preferred_element_type=f32)
        opre = jnp.dot(epre.astype(bf16), vcat, preferred_element_type=f32)
        o = (osuf + jnp.where(first2, opre[:, :128], opre[:, 128:])) / total
        mix_ref[:, cols] = jnp.where(half, o[:TOK], o[TOK:]).astype(bf16)
        return 0

    lax.fori_loop(0, H // 2, heads, 0)

    out_ref[...] = jnp.dot(mix_ref[...], wo_ref[...], preferred_element_type=f32).astype(bf16)


def layer(pos, slots, hid, pre, gain, rt, grp, place, wq, wk, wv, wo):
    vmem = pl.BlockSpec(memory_space=pltpu.VMEM)
    smem = pl.BlockSpec(memory_space=pltpu.SMEM)
    hbm = pl.BlockSpec(memory_space=pl.ANY)
    bf16 = jnp.bfloat16
    return pl.pallas_call(
        layer_kernel,
        out_shape=jax.ShapeDtypeStruct((TOK, D), bf16),
        in_specs=[smem] * 2 + [vmem] * 6 + [hbm] * 4,
        out_specs=vmem,
        scratch_shapes=[pltpu.VMEM((D, D), bf16)] * 4
        + [
            pltpu.VMEM((8, 8, 2 * D), bf16),
            pltpu.VMEM((4, 2, 8, 2 * D), bf16),
            pltpu.VMEM((KEYS, D), bf16),
            pltpu.VMEM((16, 2, 32, D), bf16),
            pltpu.VMEM((16, 2, 32, D), bf16),
            pltpu.VMEM((KEYS, D), bf16),
            pltpu.VMEM((TOK, D), bf16),
            pltpu.VMEM((KEYS, D), bf16),
            pltpu.VMEM((KEYS, D), bf16),
            pltpu.VMEM((8, TOK * H, 128), jnp.float32),
            pltpu.VMEM((4, TOK * H, 128), jnp.float32),
            pltpu.VMEM((TOK, KEYS), jnp.float32),
            pltpu.VMEM((TOK, D), bf16),
            pltpu.SemaphoreType.DMA((80,)),
            pltpu.SemaphoreType.DMA((80,)),
            pltpu.SemaphoreType.DMA((4,)),
        ],
        compiler_params=pltpu.CompilerParams(
            vmem_limit_bytes=58 << 20, collective_id=0, has_side_effects=True
        ),
        name="layer",
    )(pos, slots, hid, pre, gain, rt, grp, place, wq, wk, wv, wo)


def shards(
    hidden,
    ln_gain,
    w_query,
    w_key,
    w_value,
    w_out,
    rel_bias,
    prefix_cache,
    bucket_of_distance,
    slot_of_group,
    suffix_lengths,
    request_group,
):
    tp_index = lax.axis_index("tp")
    lens = suffix_lengths[0]
    ends = jnp.cumsum(lens)
    starts = ends - lens
    rows = tp_index * TOK + jnp.arange(TOK)
    req = jnp.minimum(jnp.sum((rows[:, None] >= ends[None, :]).astype(jnp.int32), axis=1), 127)
    onehot = req[:, None] == jnp.arange(lens.shape[0])[None, :]
    pos = rows - jnp.sum(jnp.where(onehot, starts[None, :], 0), axis=1)
    grp = jnp.sum(jnp.where(onehot, request_group[0][None, :], 0), axis=1)

    table = jnp.dot(
        rel_bias.T,
        jax.nn.one_hot(bucket_of_distance[::-1], rel_bias.shape[0], dtype=jnp.float32, axis=0),
        precision=lax.Precision.HIGHEST,
    )
    rt = jnp.pad(table, ((0, 0), (0, 128)))
    off = PREFIX - 1 - pos
    return layer(
        jnp.stack([off // 128, 127 - off % 128]),
        slot_of_group,
        hidden,
        prefix_cache.reshape(2, 8, 2 * D),
        ln_gain[None, :],
        rt,
        grp[:, None],
        pos[:, None],
        w_query,
        w_key,
        w_value,
        w_out,
    )


def solution(mesh):
    in_specs = (
        P(("grp", "tp"), None),
        P(),
        P(),
        P(),
        P(),
        P(),
        P(),
        P("grp", "tp", None, None),
        P(),
        P(),
        P("grp", None),
        P("grp", None),
    )
    out_specs = P(("grp", "tp"), None)
    return jax.shard_map(shards, mesh=mesh, in_specs=in_specs, out_specs=out_specs, check_vma=False)
```

time: 166 us -> 92.8 us (0.56)
  waiting for transfers between devices: 77.4 us -> 0 us
  Pallas kernels: 33.1 us -> 80.4 us
  starting transfers between devices: 17.3 us -> 0 us
  between operations: 13.5 us -> 0.05 us
  blocking collectives: 8.86 us -> 0 us
  local copies, waits for them, and re-layouts: 10.8 us -> 7.44 us
    all_gather x1 -> x0, waiting for transfers between devices: 66.6 us -> none  [shards(): kv = lax.all_gather(mine, 'tp', axis=1, tiled=True)]
    pallas_call x1, Pallas kernels: 33.1 us -> 80.4 us  [layer(): pl.pallas_call(layer_kernel, out_shape=jax.ShapeDtypeStruct((TOK, D), bf1...]
    ppermute x4 -> x0, starting transfers between devices: 17.3 us -> none  [shifted(): return lax.ppermute(array, axis, pairs)]
    ppermute x4 -> x0, waiting for transfers between devices: 10.8 us -> none  [shifted(): return lax.ppermute(array, axis, pairs)]
    all_gather x1 -> x0, blocking collectives: 8.86 us -> none  [shards(): owners = lax.all_gather(prefix_cache, 'grp', axis=0, tiled=True)]
    slice x1 -> x0, local copies, waits for them, and re-layouts: 2.66 us -> none  [shards(): pv = kv[:, :, :, 1].transpose(1, 0, 2, 3)]
    transpose x1 -> x0, local copies, waits for them, and re-layouts: 2.39 us -> none  [shards(): pv = kv[:, :, :, 1].transpose(1, 0, 2, 3)]
  transfers between devices with their start and end apart: 5 -> 0, of which waited for: 3 -> 0; matrix products, arithmetic and copies ran while one was open for 4% -> 0% of each run, Pallas kernels for 0% -> 0%
where the time goes in v2:
time: 92.8 us; the launch traced here: 91.2 us
  Pallas kernels  80.4 us (87%)
  local copies, waits for them, and re-layouts  7.44 us (8%)
  other arithmetic  3.2 us (3%)
    pallas_call x1, Pallas kernels, layer(): pl.pallas_call(layer_kernel, out_shape=jax.ShapeDtypeStruct((TOK, D), bf1...  80.4 us

profile of v2, /device:TPU:1, one launch (start us, length us, event | category | flops | bytes accessed | tf_op | source)
XLA Modules:
  0.0 91.2 jit_solution(12016024404767937695)
XLA Ops:
  0.0 0.0 copy-start
  0.0 1.3 %broadcast_in_dim.39.gain_ref = bf16[1,1024]{1,0:T(2,128)(2,1)} reshape(bf16[1024]{0:T(1024)(128)(2,1)} %param.13) | data formatting | bytes 4096 | tf_op jit(solution)/shard_map/broadcast_in_dim | solution.py:398
  1.3 0.8 rev.3
  2.0 0.0 copy-done
  2.0 0.2 convolution_bitcast_fusion
  2.2 0.6 pad.4.rt_ref
  2.9 1.5 %reshape.124.pre_ref = bf16[2,8,2048]{2,1,0:T(8,128)(2,1)} reshape(bf16[2,8,2,1024]{3,2,1,0:T(2,128)(2,1)} %param.19) | data formatting | bytes 131072 | tf_op jit(solution)/shard_map/reshape | solution.py:397
  4.3 0.8 copy.22
  5.1 0.2 reduce-window.4
  5.3 0.1 reduce
  5.4 0.2 convert_reduce_fusion
  5.6 0.7 fusion.2
  6.2 0.8 select_reduce_fusion
  7.1 0.6 pad_add_fusion.pos_ref
  7.7 0.7 copy.25.grp_ref
  8.4 0.1 copy.24
  8.6 0.6 add_subtract_fusion.place_ref
  9.2 80.4 %layer.1 = bf16[128,1024]{1,0:T(8,128)(2,1)} custom-call(s32[2,128]{1,0:T(2,128)} %pad_add_fusion.pos_ref, s32[8]{0:T(128)} %slot_ref.1, bf16[128,1024]{1,0:T(8,128)(2,1)} %hid_ref.1, bf16[2,8,2048]{2,1,0:T(8,128)(2,1)} %reshape.124.pre_ref, bf16[1,1024]{1,0:T(2,128)(2,1)} %broadcast_in_dim.39.gain_ref, f32[16,1152]{1,0:T(8,128)} %pad.4.rt_ref, ...), custom_call_target="tpu_custom_call" | custom-call | tf_op jit(solution)/shard_map/layer/pallas_call | solution.py:331
  89.6 1.7 %copy.27 = bf16[128,1024]{1,0:T(8,128)(2,1)} copy(bf16[128,1024]{1,0:T(8,128)(2,1)} %layer.1) | data formatting | bytes 524288
  (3 shorter events, 0.0 us)
Async XLA Ops:
  0.0 2.0 %copy-start = (f32[32,16]{0,1:T(8,128)S(1)}, f32[32,16]{0,1:T(8,128)}, u32[]{:S(2)}) copy-start(f32[32,16]{0,1:T(8,128)} %param.18) | copy-start | bytes 6148

commit v3 on v2

v3 whole, which is shorter than its diff:
```python
import jax
import jax.numpy as jnp
from jax import lax
from jax.experimental import pallas as pl
from jax.experimental.pallas import tpu as pltpu
from jax.sharding import PartitionSpec as P

D = 1024
H = 16
NB = 32
TOK = 128
LMAX = 512
KEYS = LMAX + TOK
PREFIX = 512
NEG = -1e30
MESH = pl.DeviceIdType.MESH
F32 = jnp.float32
BF16 = jnp.bfloat16
NT = (((1,), (1,)), ((), ()))


def iota(shape, dim):
    return lax.broadcasted_iota(jnp.int32, shape, dim)


def layer_kernel(
    slot_ref,
    hid_ref,
    pre_ref,
    gain_ref,
    bucket_ref,
    rel_ref,
    lens_ref,
    group_ref,
    wq_hbm,
    wk_hbm,
    wv_hbm,
    out_ref,
    wq_ref,
    wk_ref,
    wv_ref,
    own_ref,
    z_ref,
    all_ref,
    pk_ref,
    pv_ref,
    n_ref,
    q_ref,
    k_ref,
    v_ref,
    rt_ref,
    s_ref,
    b_ref,
    mask_ref,
    first_ref,
    o_ref,
    top_ref,
    sum_ref,
    at_ref,
    at_smem,
    send_sem,
    recv_sem,
    load_sem,
):
    g = lax.axis_index("grp")
    t = lax.axis_index("tp")
    y, x, z = t // 16, (t // 4) % 4, t % 4

    def tp_id(i):
        return (g, lax.rem(i + 128, 64))

    def z_id(d):
        return (g, y * 16 + x * 4 + lax.rem(z + d + 4, 4))

    def x_id(d):
        return (g, y * 16 + lax.rem(x + d + 4, 4) * 4 + z)

    def y_id(d):
        return (g, lax.rem(y + d + 4, 4) * 16 + x * 4 + z)

    used = []

    def copy(src, dst, device):
        i = len(used)
        out = pltpu.make_async_remote_copy(
            src_ref=src,
            dst_ref=dst,
            send_sem=send_sem.at[i],
            recv_sem=recv_sem.at[i],
            device_id=device,
            device_id_type=MESH,
        )
        out.start()
        used.append(out)
        return out

    row_ids = [(lax.rem(g + d, 4), t) for d in (1, 2, 3)]
    greet = row_ids + [tp_id(t + d) for d in (4, -4)]
    greet = greet + [ring(d) for ring in (x_id, y_id, z_id) for d in (1, -1)]
    barrier = pltpu.get_barrier_semaphore()
    for device in greet:
        pl.semaphore_signal(barrier, inc=1, device_id=device, device_id_type=MESH)

    loads = [
        pltpu.make_async_copy(src, dst, load_sem.at[i])
        for i, (src, dst) in enumerate([(wq_hbm, wq_ref), (wk_hbm, wk_ref), (wv_hbm, wv_ref)])
    ]
    for load in loads:
        load.start()

    def places():
        sub, lane = iota((TOK, TOK), 0), iota((TOK, TOK), 1)
        eye = sub == lane
        lens = jnp.sum(jnp.where(eye, lens_ref[...], 0).astype(F32), axis=1, keepdims=True)
        starts = jnp.sum(jnp.where(sub < lane, lens, 0.0), axis=0, keepdims=True)
        rows = (t * TOK + iota((TOK, 1), 0)).astype(F32)
        begun = starts <= rows
        place = rows - jnp.max(jnp.where(begun, starts, 0.0), axis=1, keepdims=True)
        req = jnp.sum(begun.astype(F32), axis=1, keepdims=True) - 1.0
        mine = lane.astype(F32) == req
        group = jnp.sum(
            jnp.where(mine, group_ref[...], 0).astype(F32), axis=1, keepdims=True
        )
        first_ref[...] = jnp.broadcast_to(group, (TOK, TOK))
        off = (PREFIX - 1) - jnp.sum(
            jnp.where(eye, place, 0.0), axis=0, keepdims=True
        ).astype(jnp.int32)
        off = jnp.clip(off, 0, PREFIX - 1)
        at_ref[...] = jnp.concatenate(
            [jnp.right_shift(off, 7), 127 - jnp.bitwise_and(off, 127)], axis=0
        )
        move = pltpu.make_async_copy(at_ref, at_smem, load_sem.at[3])
        move.start()
        row, col = iota((TOK, KEYS), 0), iota((TOK, KEYS), 1)
        low = LMAX + row - place.astype(jnp.int32)
        mask_ref[...] = jnp.where((col >= low) & (col <= LMAX + row), 0.0, NEG)
        move.wait()

    def table():
        flip = (iota((TOK, TOK), 0) + iota((TOK, TOK), 1) == TOK - 1).astype(BF16)
        bucket = jnp.dot(
            bucket_ref[...].astype(F32).astype(BF16), flip, preferred_element_type=F32
        ).astype(jnp.int32)
        for j in range(8):
            onehot = (iota((NB, 128), 0) == bucket[7 - j : 8 - j, :]).astype(F32)
            rt_ref[:, 128 * j : 128 * (j + 1)] = lax.dot_general(
                rel_ref[...],
                onehot,
                (((1,), (0,)), ((), ())),
                precision=lax.Precision.HIGHEST,
                preferred_element_type=F32,
            )
        rt_ref[:, 1024:] = jnp.zeros((H, 128), F32)

    def slides():
        lane = iota((H, 128), 1)

        def slide(i, _):
            for a in [i * 4 + e for e in range(4)]:
                turn = jnp.bitwise_and(a + 1, 127)
                tiles = [
                    pltpu.roll(rt_ref[:, 128 * j : 128 * (j + 1)], turn, 1) for j in range(9)
                ]
                for j in range(8):
                    s_ref[j, pl.ds(pl.multiple_of(a * H, H), H), :] = jnp.where(
                        lane < a + 1, tiles[j], tiles[j + 1]
                    )
            return 0

        lax.fori_loop(0, TOK // 4, slide, 0)

    def picks():
        turned = s_ref.reshape(8, TOK, H, 128)
        wanted = b_ref.reshape(4, TOK, H, 128)

        def pick(i, _):
            for a in [i * 8 + e for e in range(8)]:
                for j in range(4):
                    wanted[j, a] = turned[at_smem[0, a] + j, at_smem[1, a]]
            return 0

        lax.fori_loop(0, TOK // 8, pick, 0)

    gain = jnp.concatenate([gain_ref[j : j + 1, :].astype(F32) for j in range(8)], axis=1)

    def norms(i):
        h = all_ref[i].astype(F32)
        ms = jnp.mean(h * h, axis=1, keepdims=True)
        n_ref[i] = (h * lax.rsqrt(ms + 1e-06) * gain).astype(BF16)

    def projects(blocks, pairs):
        for w_ref, dst_ref in pairs:

            def project(i, _):
                cols = pl.ds(pl.multiple_of(i * 256, 256), 256)
                n = jnp.concatenate([n_ref[b] for b in blocks], axis=0)
                r = jnp.dot(n, w_ref[:, cols], preferred_element_type=F32).astype(BF16)
                for j, b in enumerate(blocks):
                    dst_ref[b, :, cols] = r[TOK * j : TOK * (j + 1)]
                return 0

            lax.fori_loop(0, D // 256, project, 0)

    half = iota((TOK, 128), 1) < 64

    def stacked(cols):
        q = q_ref[4, :, cols].astype(F32)
        return jnp.concatenate([jnp.where(half, q, 0.0), jnp.where(half, 0.0, q)], axis=0)

    def gather(ref, p, tiles):
        return jnp.concatenate(
            [
                jnp.concatenate(
                    [ref[j, pl.ds(2 * p + e, TOK, stride=H), :] for j in tiles], axis=1
                )
                for e in range(2)
            ],
            axis=0,
        )

    def suffix():
        def heads(p, _):
            cols = pl.ds(pl.multiple_of(p * 128, 128), 128)
            qq = stacked(cols).astype(BF16)
            mask = mask_ref[...]
            keys = k_ref[:, :, cols].reshape(KEYS, 128)
            values = v_ref[:, :, cols].reshape(KEYS, 128)
            scores = (
                lax.dot_general(qq, keys, NT, preferred_element_type=F32)
                + gather(s_ref, p, range(3, 8))
                + jnp.concatenate([mask, mask], axis=0)
            )
            top = jnp.max(scores, axis=1, keepdims=True)
            e = jnp.exp(scores - top)
            top_ref[p] = jnp.broadcast_to(top, (2 * TOK, 128))
            sum_ref[p] = jnp.broadcast_to(jnp.sum(e, axis=1, keepdims=True), (2 * TOK, 128))
            o_ref[p] = jnp.dot(e.astype(BF16), values, preferred_element_type=F32)
            return 0

        lax.fori_loop(0, H // 2, heads, 0)

    def prefix():
        first = first_ref[...] == 0.0
        first2 = jnp.concatenate([first, first], axis=0)

        def heads(p, _):
            cols = pl.ds(pl.multiple_of(p * 128, 128), 128)
            qq = stacked(cols)
            qg = jnp.concatenate(
                [jnp.where(first2, qq, 0.0), jnp.where(first2, 0.0, qq)], axis=1
            ).astype(BF16)
            keys, values = [
                jnp.concatenate(
                    [ref[:, s, :, cols].reshape(PREFIX, 128) for s in range(2)], axis=1
                )
                for ref in (pk_ref, pv_ref)
            ]
            scores = lax.dot_general(
                qg, keys, NT, preferred_element_type=F32
            ) + gather(b_ref, p, range(4))
            old = top_ref[p]
            top = jnp.maximum(old, jnp.max(scores, axis=1, keepdims=True))
            e = jnp.exp(scores - top[:, :1])
            scale = jnp.exp(old - top)
            total = sum_ref[p] * scale + jnp.sum(e, axis=1, keepdims=True)
            o = jnp.dot(e.astype(BF16), values, preferred_element_type=F32)
            o = jnp.where(first2, o[:, :128], o[:, 128:])
            o = (o_ref[p] * scale + o) / total
            out_ref[:, cols] = jnp.where(half, o[:TOK], o[TOK:]).astype(BF16)
            return 0

        lax.fori_loop(0, H // 2, heads, 0)

    all_ref[4] = hid_ref[...]
    own_ref[pl.ds(2 * g, 2)] = pre_ref[...]
    pl.semaphore_wait(barrier, len(greet))

    rows = [copy(pre_ref, own_ref.at[pl.ds(2 * g, 2)], device) for device in row_ids]
    back4 = copy(hid_ref, all_ref.at[0], tp_id(t + 4))
    table()
    for c in rows:
        c.wait_recv()
    for s in range(2):
        slot = jnp.full((8, 2, D), slot_ref[2 * g + s], jnp.int32)
        chosen = own_ref[0].astype(F32)
        for i in range(1, 8):
            chosen = jnp.where(slot == i, own_ref[i].astype(F32), chosen)
        z_ref[z, s] = jnp.concatenate([chosen[:, 0, :], chosen[:, 1, :]], axis=1).astype(BF16)

    def spread(buf, piece, me, ring):
        part = buf.at[piece(me)]
        return [copy(part, part, ring(1)), copy(part, part, ring(-1))]

    def onward(buf, piece, me, ring, first, step):
        first[0 if step == 1 else 1].wait_recv()
        part = buf.at[piece(lax.rem(me - step + 4, 4))]
        return copy(part, part, ring(step))

    zs = [spread(z_ref, lambda i, s=s: (i, s), z, z_id) for s in range(2)]
    slides()
    zfwd = [
        onward(z_ref, lambda i, s=s: (i, s), z, z_id, zs[s], 1 - 2 * s) for s in range(2)
    ]
    back4.wait_recv()
    up = copy(all_ref.at[4 - 4 * ((z + 1) // 4)], all_ref.at[3], z_id(1))
    down = copy(all_ref.at[4 * ((4 - z) // 4)], all_ref.at[1], z_id(-1))
    places()
    zs[0][1].wait_recv()
    zs[1][0].wait_recv()
    for c in zfwd:
        c.wait_recv()

    for s in range(2):
        for i in range(2):
            both = jnp.concatenate(
                [z_ref[2 * i, s].astype(F32), z_ref[2 * i + 1, s].astype(F32)], axis=0
            ).astype(BF16)
            pk_ref[y * 4 + x, s, 16 * i : 16 * (i + 1), :] = both[:, :D]
            pv_ref[y * 4 + x, s, 16 * i : 16 * (i + 1), :] = both[:, D:]

    def at_x(i, other, s):
        return (other * 4 + i, s)

    def at_y(i, other, s):
        return (i * 4 + other, s)

    lines = []
    for s in range(2):
        lines.append((pk_ref, s, x, y, x_id, y_id, at_x, at_y))
        lines.append((pv_ref, s, y, x, y_id, x_id, at_y, at_x))
    one = []
    for buf, s, me, other, ring, _, at, _ in lines:
        one.append(spread(buf, lambda i, s=s, at=at, o=other: at(i, o, s), me, ring))

    def second(line, shift):
        buf, s, me, other, _, ring, _, at = line
        chunk = lax.rem(me + shift + 4, 4)
        return spread(buf, lambda i: at(i, chunk, s), other, ring)

    def second_on(line, shift, first):
        buf, s, me, other, _, ring, _, at = line
        chunk = lax.rem(me + shift + 4, 4)
        step = 1 - 2 * s
        return onward(buf, lambda i: at(i, chunk, s), other, ring, first, step)

    two = [{0: second(line, 0)} for line in lines]
    norms(4)
    for load in loads:
        load.wait()
    projects((4,), [(wq_ref, q_ref), (wk_ref, k_ref), (wv_ref, v_ref)])
    far = []
    for line, first, rest in zip(lines, one, two):
        buf, s, me, other, ring, _, at, _ = line
        step = 1 - 2 * s
        far.append(onward(buf, lambda i: at(i, other, s), me, ring, first, step))
        rest[-step] = second(line, -step)
    for line, first, rest in zip(lines, one, two):
        step = 1 - 2 * line[1]
        first[1 if step == 1 else 0].wait_recv()
        rest[step] = second(line, step)

    picks()
    last = [second_on(line, 0, rest[0]) for line, rest in zip(lines, two)]
    for line, rest, c in zip(lines, two, far):
        c.wait_recv()
        rest[2] = second(line, 2)

    up.wait_recv()
    down.wait_recv()
    odd = lax.rem(z, 2)
    back2 = copy(all_ref.at[3 - 2 * odd], all_ref.at[2], z_id(1 - 2 * odd))
    for i in (0, 1, 3):
        norms(i)
    projects((0, 1, 3), [(wk_ref, k_ref), (wv_ref, v_ref)])
    for shift in (1, -1, 2):
        last = last + [
            second_on(line, shift, rest[shift]) for line, rest in zip(lines, two)
        ]
    back2.wait_recv()
    norms(2)
    projects((2,), [(wk_ref, k_ref), (wv_ref, v_ref)])
    suffix()
    for line, rest in zip(lines, two):
        step = 1 - 2 * line[1]
        for shift in (0, 1, -1, 2):
            rest[shift][1 if step == 1 else 0].wait_recv()
    for c in last:
        c.wait_recv()
    prefix()
    for c in used:
        c.wait_send()


def layer(slots, hid, pre, gain, bucket, rel, lens, group, wq, wk, wv):
    vmem = pl.BlockSpec(memory_space=pltpu.VMEM)
    smem = pl.BlockSpec(memory_space=pltpu.SMEM)
    hbm = pl.BlockSpec(memory_space=pl.ANY)
    pair = pltpu.VMEM((H // 2, 2 * TOK, 128), F32)
    return pl.pallas_call(
        layer_kernel,
        out_shape=jax.ShapeDtypeStruct((TOK, D), BF16),
        in_specs=[smem] + [vmem] * 7 + [hbm] * 3,
        out_specs=vmem,
        scratch_shapes=[pltpu.VMEM((D, D), BF16)] * 3
        + [
            pltpu.VMEM((8, 8, 2, D), BF16),
            pltpu.VMEM((4, 2, 8, 2 * D), BF16),
            pltpu.VMEM((5, TOK, D), BF16),
            pltpu.VMEM((16, 2, 32, D), BF16),
            pltpu.VMEM((16, 2, 32, D), BF16),
            pltpu.VMEM((5, TOK, D), BF16),
            pltpu.VMEM((5, TOK, D), BF16),
            pltpu.VMEM((5, TOK, D), BF16),
            pltpu.VMEM((5, TOK, D), BF16),
            pltpu.VMEM((H, 1152), F32),
            pltpu.VMEM((8, TOK * H, 128), F32),
            pltpu.VMEM((4, TOK * H, 128), F32),
            pltpu.VMEM((TOK, KEYS), F32),
            pltpu.VMEM((TOK, TOK), F32),
            pair,
            pair,
            pair,
            pltpu.VMEM((2, TOK), jnp.int32),
            pltpu.SMEM((2, TOK), jnp.int32),
            pltpu.SemaphoreType.DMA((80,)),
            pltpu.SemaphoreType.DMA((80,)),
            pltpu.SemaphoreType.DMA((4,)),
        ],
        compiler_params=pltpu.CompilerParams(
            vmem_limit_bytes=58 << 20, collective_id=0, has_side_effects=True
        ),
        name="layer",
    )(slots, hid, pre, gain, bucket, rel, lens, group, wq, wk, wv)


def shards(
    hidden,
    ln_gain,
    w_query,
    w_key,
    w_value,
    w_out,
    rel_bias,
    prefix_cache,
    bucket_of_distance,
    slot_of_group,
    suffix_lengths,
    request_group,
):
    mixed = layer(
        slot_of_group,
        hidden,
        prefix_cache,
        ln_gain.reshape(8, 128),
        bucket_of_distance.reshape(8, 128),
        rel_bias.T,
        suffix_lengths,
        request_group,
        w_query,
        w_key,
        w_value,
    )
    return jnp.dot(mixed, w_out, preferred_element_type=jnp.float32).astype(jnp.bfloat16)


def solution(mesh):
    in_specs = (
        P(("grp", "tp"), None),
        P(),
        P(),
        P(),
        P(),
        P(),
        P(),
        P("grp", "tp", None, None),
        P(),
        P(),
        P("grp", None),
        P("grp", None),
    )
    out_specs = P(("grp", "tp"), None)
    return jax.shard_map(shards, mesh=mesh, in_specs=in_specs, out_specs=out_specs, check_vma=False)
```

time: 92.8 us -> 70.4 us (0.76); the launches traced: 91.2 us -> 70.3 us
  Pallas kernels: 80.4 us -> 68.2 us
  local copies, waits for them, and re-layouts: 7.44 us -> 0.01 us
  other arithmetic: 3.2 us -> 0 us
  matrix products: 0.17 us -> 2.1 us
    pallas_call x1, Pallas kernels: 80.4 us -> 68.2 us  [layer(): pl.pallas_call(layer_kernel, out_shape=jax.ShapeDtypeStruct((TOK, D), BF1...]
    reshape x2 -> x0, local copies, waits for them, and re-layouts: 2.25 us -> none  [the longest x1 1.49 us: shards(): prefix_cache.reshape(2, 8, 2 * D)]
    broadcast_in_dim x2 -> x0, local copies, waits for them, and re-layouts: 2.01 us -> none  [the longest x1 1.27 us: shards(): ln_gain[None, :]]
    dot_general x1, matrix products: 0.17 us -> 2.1 us  [shards(): jnp.dot(mixed, w_out, preferred_element_type=jnp.float32)]
    unnamed x3 -> x2, local copies, waits for them, and re-layouts: 1.67 us -> 0.01 us
    reduce_sum x2 -> x0, other arithmetic: 1 us -> none  [the longest x1 0.82 us: shards(): grp = jnp.sum(jnp.where(onehot, request_group[0][None, :], 0), axis=1)]
where the time goes in v3:
time: 70.4 us; the launch traced here: 70.3 us
  Pallas kernels  68.2 us (97%)
  matrix products  2.1 us (3%)
    pallas_call x1, Pallas kernels, layer(): pl.pallas_call(layer_kernel, out_shape=jax.ShapeDtypeStruct((TOK, D), BF1...  68.2 us
    dot_general x1, matrix products, shards(): jnp.dot(mixed, w_out, preferred_element_type=jnp.float32)  2.1 us

profile of v3, /device:TPU:1, one launch (start us, length us, event | category | flops | bytes accessed | tf_op | source)
XLA Modules:
  0.0 70.3 jit_solution(12576544559220601621)
XLA Ops:
  0.0 0.0 copy-start
  0.0 68.2 %layer.1 = bf16[128,1024]{1,0:T(8,128)(2,1)} custom-call(s32[8]{0:T(128)} %slot_ref.1, bf16[128,1024]{1,0:T(8,128)(2,1)} %hid_ref.1, bf16[2,8,2,1024]{3,2,1,0:T(2,128)(2,1)} %pre_ref.1, bf16[8,128]{1,0:T(8,128)(2,1)} %bitcast.7, s32[8,128]{1,0:T(8,128)} %bitcast.6, f32[16,32]{1,0:T(8,128)} %bitcast.5, s32[1,128]{1,0:T(1,128)} %lens_ref.1, ...), custom_call_target="tpu_custom_call" | custom-call | tf_op jit(solution)/shard_map/layer/pallas_call | solution.py:399
  68.2 0.0 copy-done
  68.2 2.1 %convolution_convert_fusion = bf16[128,1024]{1,0:T(8,128)(2,1)} fusion(bf16[128,1024]{1,0:T(8,128)(2,1)} %layer.1, bf16[1024,1024]{1,0:T(8,128)(2,1)S(1)} %copy-done), kind=kOutput, calls=%fused_computation | convolution fusion | flops 268566528 | bytes 2621440 | tf_op jit(solution)/shard_map/dot_general | solution.py:463
Async XLA Ops:
  0.0 68.2 %copy-start = (bf16[1024,1024]{1,0:T(8,128)(2,1)S(1)}, bf16[1024,1024]{1,0:T(8,128)(2,1)}, u32[]{:S(2)}) copy-start(bf16[1024,1024]{1,0:T(8,128)(2,1)} %param.17) | copy-start | bytes 6291460

commit v4 on v3

--- a/solution.py
+++ b/solution.py
@@ -16,6 +16,7 @@
 MESH = pl.DeviceIdType.MESH
 F32 = jnp.float32
 BF16 = jnp.bfloat16
+UNROLL = 4
 NT = (((1,), (1,)), ((), ()))
 
 
@@ -131,9 +132,11 @@
         )
         move = pltpu.make_async_copy(at_ref, at_smem, load_sem.at[3])
         move.start()
-        row, col = iota((TOK, KEYS), 0), iota((TOK, KEYS), 1)
+        row, col = iota((TOK, 128), 0), iota((TOK, 128), 1)
         low = LMAX + row - place.astype(jnp.int32)
-        mask_ref[...] = jnp.where((col >= low) & (col <= LMAX + row), 0.0, NEG)
+        for j in range(5):
+            at = col + 128 * j
+            mask_ref[j] = jnp.where((at >= low) & (at <= LMAX + row), 0.0, NEG)
         move.wait()
 
     def table():
@@ -152,7 +155,7 @@
             )
         rt_ref[:, 1024:] = jnp.zeros((H, 128), F32)
 
-    def slides():
+    def slides(start, stop):
         lane = iota((H, 128), 1)
 
         def slide(i, _):
@@ -167,7 +170,7 @@
                     )
             return 0
 
-        lax.fori_loop(0, TOK // 4, slide, 0)
+        lax.fori_loop(start // 4, stop // 4, slide, 0)
 
     def picks():
         turned = s_ref.reshape(8, TOK, H, 128)
@@ -218,175 +221,230 @@
             axis=0,
         )
 
-    def suffix():
+    def update(p, sets, begin, end):
+        wide = (2 * TOK, 128)
+        tops = [jnp.max(scores, axis=1, keepdims=True) for scores, _, _ in sets]
+        top = jnp.broadcast_to(tops[0] if len(tops) == 1 else jnp.maximum(*tops), wide)
+        if not begin:
+            old = top_ref[p]
+            top = jnp.maximum(old, top)
+            scale = jnp.exp(old - top)
+        total, o = 0.0, 0.0
+        for scores, values, first2 in sets:
+            e = jnp.exp(scores - jnp.concatenate([top] * (scores.shape[1] // 128), axis=1))
+            total = total + jnp.broadcast_to(jnp.sum(e, axis=1, keepdims=True), wide)
+            part = jnp.dot(e.astype(BF16), values, preferred_element_type=F32)
+            if first2 is not None:
+                part = jnp.where(first2, part[:, :128], part[:, 128:])
+            o = o + part
+        if not begin:
+            total = sum_ref[p] * scale + total
+            o = o_ref[p] * scale + o
+        if end:
+            o = o / total
+            cols = pl.ds(pl.multiple_of(p * 128, 128), 128)
+            out_ref[:, cols] = jnp.where(half, o[:TOK], o[TOK:]).astype(BF16)
+        else:
+            top_ref[p] = top
+            sum_ref[p] = total
+            o_ref[p] = o
+
+    def suffix_set(p, blocks):
+        cols = pl.ds(pl.multiple_of(p * 128, 128), 128)
+        keys, values = [
+            jnp.concatenate([ref[b, :, cols] for b in blocks], axis=0) for ref in (k_ref, v_ref)
+        ]
+        mask = jnp.concatenate([mask_ref[b] for b in blocks], axis=1)
+        scores = (
+            lax.dot_general(stacked(cols).astype(BF16), keys, NT, preferred_element_type=F32)
+            + gather(s_ref, p, [b + 3 for b in blocks])
+            + jnp.concatenate([mask, mask], axis=0)
+        )
+        return scores, values, None
+
+    def prefix_set(p, h, i, first2):
+        part = pl.ds(pl.multiple_of(i * 128, 128), 128)
+        qq = stacked(pl.ds(pl.multiple_of(p * 128, 128), 128))
+        qg = jnp.concatenate(
+            [jnp.where(first2, qq, 0.0), jnp.where(first2, 0.0, qq)], axis=1
+        ).astype(BF16)
+        keys, values = [
+            jnp.concatenate(
+                [ref[h, :, s, :, part].reshape(PREFIX, 128) for s in range(2)], axis=1
+            )
+            for ref in (pk_ref, pv_ref)
+        ]
+        scores = lax.dot_general(qg, keys, NT, preferred_element_type=F32)
+        return scores + gather(b_ref, p, range(4)), values, first2
+
+    def suffix(blocks, start, stop, begin, end):
         def heads(p, _):
-            cols = pl.ds(pl.multiple_of(p * 128, 128), 128)
-            qq = stacked(cols).astype(BF16)
-            mask = mask_ref[...]
-            keys = k_ref[:, :, cols].reshape(KEYS, 128)
-            values = v_ref[:, :, cols].reshape(KEYS, 128)
-            scores = (
-                lax.dot_general(qq, keys, NT, preferred_element_type=F32)
-                + gather(s_ref, p, range(3, 8))
-                + jnp.concatenate([mask, mask], axis=0)
-            )
-            top = jnp.max(scores, axis=1, keepdims=True)
-            e = jnp.exp(scores - top)
-            top_ref[p] = jnp.broadcast_to(top, (2 * TOK, 128))
-            sum_ref[p] = jnp.broadcast_to(jnp.sum(e, axis=1, keepdims=True), (2 * TOK, 128))
-            o_ref[p] = jnp.dot(e.astype(BF16), values, preferred_element_type=F32)
+            update(p, [suffix_set(p, blocks)], begin, end)
             return 0
 
-        lax.fori_loop(0, H // 2, heads, 0)
-
-    def prefix():
-        first = first_ref[...] == 0.0
-        first2 = jnp.concatenate([first, first], axis=0)
-
-        def heads(p, _):
-            cols = pl.ds(pl.multiple_of(p * 128, 128), 128)
-            qq = stacked(cols)
-            qg = jnp.concatenate(
-                [jnp.where(first2, qq, 0.0), jnp.where(first2, 0.0, qq)], axis=1
-            ).astype(BF16)
-            keys, values = [
-                jnp.concatenate(
-                    [ref[:, s, :, cols].reshape(PREFIX, 128) for s in range(2)], axis=1
-                )
-                for ref in (pk_ref, pv_ref)
-            ]
-            scores = lax.dot_general(
-                qg, keys, NT, preferred_element_type=F32
-            ) + gather(b_ref, p, range(4))
-            old = top_ref[p]
-            top = jnp.maximum(old, jnp.max(scores, axis=1, keepdims=True))
-            e = jnp.exp(scores - top[:, :1])
-            scale = jnp.exp(old - top)
-            total = sum_ref[p] * scale + jnp.sum(e, axis=1, keepdims=True)
-            o = jnp.dot(e.astype(BF16), values, preferred_element_type=F32)
-            o = jnp.where(first2, o[:, :128], o[:, 128:])
-            o = (o_ref[p] * scale + o) / total
-            out_ref[:, cols] = jnp.where(half, o[:TOK], o[TOK:]).astype(BF16)
+        lax.fori_loop(start, stop, heads, 0, unroll=UNROLL)
+
+    def prefix(h, blocks, end):
+        def heads(i, _):
+            first = first_ref[...] == 0.0
+            first2 = jnp.concatenate([first, first], axis=0)
+            p = 4 * h + i
+            sets = [prefix_set(p, h, i, first2)]
+            if blocks:
+                sets.append(suffix_set(p, blocks))
+            update(p, sets, False, end)
             return 0
 
-        lax.fori_loop(0, H // 2, heads, 0)
+        lax.fori_loop(0, 4, heads, 0, unroll=UNROLL)
 
     all_ref[4] = hid_ref[...]
-    own_ref[pl.ds(2 * g, 2)] = pre_ref[...]
+    mine = pl.ds(2 * g, 2)
+    for i in range(2):
+        raw = pre_ref[i].astype(F32)
+        own_ref[2 * g + i] = jnp.concatenate([raw[:, 0, :], raw[:, 1, :]], axis=1).astype(BF16)
+    table()
+    places()
     pl.semaphore_wait(barrier, len(greet))
 
-    rows = [copy(pre_ref, own_ref.at[pl.ds(2 * g, 2)], device) for device in row_ids]
+    rows = [copy(own_ref.at[mine], own_ref.at[mine], device) for device in row_ids]
     back4 = copy(hid_ref, all_ref.at[0], tp_id(t + 4))
-    table()
+    slides(0, TOK // 2)
     for c in rows:
         c.wait_recv()
-    for s in range(2):
-        slot = jnp.full((8, 2, D), slot_ref[2 * g + s], jnp.int32)
-        chosen = own_ref[0].astype(F32)
-        for i in range(1, 8):
-            chosen = jnp.where(slot == i, own_ref[i].astype(F32), chosen)
-        z_ref[z, s] = jnp.concatenate([chosen[:, 0, :], chosen[:, 1, :]], axis=1).astype(BF16)
-
-    def spread(buf, piece, me, ring):
-        part = buf.at[piece(me)]
+    for i in range(2):
+        z_ref[z, i] = own_ref[slot_ref[2 * g + i]]
+
+    def spread(part, ring):
         return [copy(part, part, ring(1)), copy(part, part, ring(-1))]
 
-    def onward(buf, piece, me, ring, first, step):
-        first[0 if step == 1 else 1].wait_recv()
-        part = buf.at[piece(lax.rem(me - step + 4, 4))]
-        return copy(part, part, ring(step))
-
-    zs = [spread(z_ref, lambda i, s=s: (i, s), z, z_id) for s in range(2)]
-    slides()
-    zfwd = [
-        onward(z_ref, lambda i, s=s: (i, s), z, z_id, zs[s], 1 - 2 * s) for s in range(2)
-    ]
-    back4.wait_recv()
-    up = copy(all_ref.at[4 - 4 * ((z + 1) // 4)], all_ref.at[3], z_id(1))
-    down = copy(all_ref.at[4 * ((4 - z) // 4)], all_ref.at[1], z_id(-1))
-    places()
-    zs[0][1].wait_recv()
-    zs[1][0].wait_recv()
-    for c in zfwd:
-        c.wait_recv()
-
-    for s in range(2):
-        for i in range(2):
-            both = jnp.concatenate(
-                [z_ref[2 * i, s].astype(F32), z_ref[2 * i + 1, s].astype(F32)], axis=0
-            ).astype(BF16)
-            pk_ref[y * 4 + x, s, 16 * i : 16 * (i + 1), :] = both[:, :D]
-            pv_ref[y * 4 + x, s, 16 * i : 16 * (i + 1), :] = both[:, D:]
-
-    def at_x(i, other, s):
-        return (other * 4 + i, s)
-
-    def at_y(i, other, s):
-        return (i * 4 + other, s)
-
-    lines = []
-    for s in range(2):
-        lines.append((pk_ref, s, x, y, x_id, y_id, at_x, at_y))
-        lines.append((pv_ref, s, y, x, y_id, x_id, at_y, at_x))
-    one = []
-    for buf, s, me, other, ring, _, at, _ in lines:
-        one.append(spread(buf, lambda i, s=s, at=at, o=other: at(i, o, s), me, ring))
-
-    def second(line, shift):
-        buf, s, me, other, _, ring, _, at = line
-        chunk = lax.rem(me + shift + 4, 4)
-        return spread(buf, lambda i: at(i, chunk, s), other, ring)
-
-    def second_on(line, shift, first):
-        buf, s, me, other, _, ring, _, at = line
-        chunk = lax.rem(me + shift + 4, 4)
-        step = 1 - 2 * s
-        return onward(buf, lambda i: at(i, chunk, s), other, ring, first, step)
-
-    two = [{0: second(line, 0)} for line in lines]
+    def onward(part, me, ring, first):
+        out = []
+        for i, step in ((0, 1), (1, -1)):
+            first[i].wait_recv()
+            piece = part(lax.rem(me - step + 4, 4)).at[i]
+            out.append(copy(piece, piece, ring(step)))
+        return out
+
+    own = z_ref.at[z]
+    ahead = [copy(own.at[i], own.at[i], z_id(1 - 2 * i)) for i in range(2)]
+    rest = [copy(own.at[i], own.at[i], z_id(2 * i - 1)) for i in range(2)]
+    slides(TOK // 2, TOK)
+    zfwd = onward(lambda i: z_ref.at[i], z, z_id, ahead)
     norms(4)
     for load in loads:
         load.wait()
     projects((4,), [(wq_ref, q_ref), (wk_ref, k_ref), (wv_ref, v_ref)])
-    far = []
-    for line, first, rest in zip(lines, one, two):
-        buf, s, me, other, ring, _, at, _ = line
-        step = 1 - 2 * s
-        far.append(onward(buf, lambda i: at(i, other, s), me, ring, first, step))
-        rest[-step] = second(line, -step)
-    for line, first, rest in zip(lines, one, two):
-        step = 1 - 2 * line[1]
-        first[1 if step == 1 else 0].wait_recv()
-        rest[step] = second(line, step)
+    for c in rest + zfwd:
+        c.wait_recv()
+
+    def place_own(h):
+        for i in range(2):
+            for j in range(2):
+                both = jnp.concatenate(
+                    [z_ref[2 * j, i].astype(F32), z_ref[2 * j + 1, i].astype(F32)], axis=0
+                ).astype(BF16)
+                low = D // 2 * h
+                rows = slice(16 * j, 16 * (j + 1))
+                pk_ref[h, y * 4 + x, i, rows, :] = both[:, low : low + D // 2]
+                pv_ref[h, y * 4 + x, i, rows, :] = both[:, D + low : D + low + D // 2]
+
+    def line(h, swap):
+        buf = (pv_ref if swap else pk_ref).at[h]
+        me, other = (y, x) if swap else (x, y)
+        ring, ring2 = (y_id, x_id) if swap else (x_id, y_id)
+
+        def at(i, j):
+            return buf.at[i * 4 + j] if swap else buf.at[j * 4 + i]
+
+        state = {}
+
+        def start():
+            state["one"] = spread(at(me, other), ring)
+            state[0] = spread(at(me, other), ring2)
+
+        def second(shift):
+            state[shift] = spread(at(lax.rem(me + shift + 4, 4), other), ring2)
+
+        def turn():
+            state["far"] = onward(lambda i: at(i, other), me, ring, state["one"])
+            second(-1)
+            second(1)
+
+        def last():
+            for c in state["far"]:
+                c.wait_recv()
+            second(2)
+
+        def on(shift):
+            state[shift, 2] = onward(
+                lambda j: at(lax.rem(me + shift + 4, 4), j), other, ring2, state[shift]
+            )
+
+        def done():
+            for shift in (0, -1, 1, 2):
+                for c in state[shift, 2]:
+                    c.wait_recv()
+
+        return dict(start=start, turn=turn, last=last, on=on, done=done)
+
+    lines = [[line(h, False), line(h, True)] for h in range(2)]
+
+    def run(h, name, *args):
+        for item in lines[h]:
+            item[name](*args)
+
+    for h in range(2):
+        place_own(h)
+        run(h, "start")
+    back4.wait_recv()
+    from_up, from_down = 4 - 4 * ((z + 1) // 4), 4 * ((4 - z) // 4)
+    odd = lax.rem(z, 2)
+    parts = [pl.ds(TOK // 2 * i, TOK // 2) for i in range(2)]
+    near = [
+        [
+            copy(all_ref.at[from_up, part], all_ref.at[3, part], z_id(1)),
+            copy(all_ref.at[from_down, part], all_ref.at[1, part], z_id(-1)),
+        ]
+        for part in parts
+    ]
+
+    def two_back(i):
+        for c in near[i]:
+            c.wait_recv()
+        return copy(
+            all_ref.at[3 - 2 * odd, parts[i]], all_ref.at[2, parts[i]], z_id(1 - 2 * odd)
+        )
 
     picks()
-    last = [second_on(line, 0, rest[0]) for line, rest in zip(lines, two)]
-    for line, rest, c in zip(lines, two, far):
+    run(0, "turn")
+    run(1, "turn")
+    norms(0)
+    run(0, "on", 0)
+    run(0, "last")
+    back2 = [two_back(0)]
+    run(1, "on", 0)
+    run(1, "last")
+    back2.append(two_back(1))
+    norms(1)
+    norms(3)
+    projects((0, 1, 3), [(wk_ref, k_ref), (wv_ref, v_ref)])
+    run(0, "on", -1)
+    run(0, "on", 1)
+    suffix((0, 1, 3, 4), 0, 4, True, False)
+    run(1, "on", -1)
+    run(1, "on", 1)
+    run(0, "on", 2)
+    suffix((0, 1, 3, 4), 4, 8, True, False)
+    run(1, "on", 2)
+    run(0, "done")
+    prefix(0, (), False)
+    for c in back2:
         c.wait_recv()
-        rest[2] = second(line, 2)
-
-    up.wait_recv()
-    down.wait_recv()
-    odd = lax.rem(z, 2)
-    back2 = copy(all_ref.at[3 - 2 * odd], all_ref.at[2], z_id(1 - 2 * odd))
-    for i in (0, 1, 3):
-        norms(i)
-    projects((0, 1, 3), [(wk_ref, k_ref), (wv_ref, v_ref)])
-    for shift in (1, -1, 2):
-        last = last + [
-            second_on(line, shift, rest[shift]) for line, rest in zip(lines, two)
-        ]
-    back2.wait_recv()
     norms(2)
     projects((2,), [(wk_ref, k_ref), (wv_ref, v_ref)])
-    suffix()
-    for line, rest in zip(lines, two):
-        step = 1 - 2 * line[1]
-        for shift in (0, 1, -1, 2):
-            rest[shift][1 if step == 1 else 0].wait_recv()
-    for c in last:
-        c.wait_recv()
-    prefix()
+    suffix((2,), 0, 4, False, True)
+    run(1, "done")
+    prefix(1, (2,), True)
     for c in used:
         c.wait_send()
 
@@ -403,11 +461,11 @@
         out_specs=vmem,
         scratch_shapes=[pltpu.VMEM((D, D), BF16)] * 3
         + [
-            pltpu.VMEM((8, 8, 2, D), BF16),
+            pltpu.VMEM((8, 8, 2 * D), BF16),
             pltpu.VMEM((4, 2, 8, 2 * D), BF16),
             pltpu.VMEM((5, TOK, D), BF16),
-            pltpu.VMEM((16, 2, 32, D), BF16),
-            pltpu.VMEM((16, 2, 32, D), BF16),
+            pltpu.VMEM((2, 16, 2, 32, D // 2), BF16),
+            pltpu.VMEM((2, 16, 2, 32, D // 2), BF16),
             pltpu.VMEM((5, TOK, D), BF16),
             pltpu.VMEM((5, TOK, D), BF16),
             pltpu.VMEM((5, TOK, D), BF16),
@@ -415,15 +473,15 @@
             pltpu.VMEM((H, 1152), F32),
             pltpu.VMEM((8, TOK * H, 128), F32),
             pltpu.VMEM((4, TOK * H, 128), F32),
-            pltpu.VMEM((TOK, KEYS), F32),
+            pltpu.VMEM((5, TOK, 128), F32),
             pltpu.VMEM((TOK, TOK), F32),
             pair,
             pair,
             pair,
             pltpu.VMEM((2, TOK), jnp.int32),
             pltpu.SMEM((2, TOK), jnp.int32),
-            pltpu.SemaphoreType.DMA((80,)),
-            pltpu.SemaphoreType.DMA((80,)),
+            pltpu.SemaphoreType.DMA((104,)),
+            pltpu.SemaphoreType.DMA((104,)),
             pltpu.SemaphoreType.DMA((4,)),
         ],
         compiler_params=pltpu.CompilerParams(

time: 70.4 us -> 60.8 us (0.86)
  Pallas kernels: 68.2 us -> 58.1 us
    pallas_call x1, Pallas kernels: 68.2 us -> 58.1 us  [layer(): pl.pallas_call(layer_kernel, out_shape=jax.ShapeDtypeStruct((TOK, D), BF1...]
where the time goes in v4:
time: 60.8 us; the launch traced here: 60.2 us
  Pallas kernels  58.1 us (96%)
  matrix products  2.1 us (3%)
    pallas_call x1, Pallas kernels, layer(): pl.pallas_call(layer_kernel, out_shape=jax.ShapeDtypeStruct((TOK, D), BF1...  58.1 us
    dot_general x1, matrix products, shards(): jnp.dot(mixed, w_out, preferred_element_type=jnp.float32)  2.1 us

profile of v4, /device:TPU:1, one launch (start us, length us, event | category | flops | bytes accessed | tf_op | source)
XLA Modules:
  0.0 60.2 jit_solution(1281117258485182354)
XLA Ops:
  0.0 0.0 copy-start
  0.0 58.1 %layer.1 = bf16[128,1024]{1,0:T(8,128)(2,1)} custom-call(s32[8]{0:T(128)} %slot_ref.1, bf16[128,1024]{1,0:T(8,128)(2,1)} %hid_ref.1, bf16[2,8,2,1024]{3,2,1,0:T(2,128)(2,1)} %pre_ref.1, bf16[8,128]{1,0:T(8,128)(2,1)} %bitcast.7, s32[8,128]{1,0:T(8,128)} %bitcast.6, f32[16,32]{1,0:T(8,128)} %bitcast.5, s32[1,128]{1,0:T(1,128)} %lens_ref.1, ...), custom_call_target="tpu_custom_call" | custom-call | tf_op jit(solution)/shard_map/layer/pallas_call | solution.py:457
  58.1 0.0 copy-done
  58.1 2.1 %convolution_convert_fusion = bf16[128,1024]{1,0:T(8,128)(2,1)} fusion(bf16[128,1024]{1,0:T(8,128)(2,1)} %layer.1, bf16[1024,1024]{1,0:T(8,128)(2,1)S(1)} %copy-done), kind=kOutput, calls=%fused_computation | convolution fusion | flops 268566528 | bytes 2621440 | tf_op jit(solution)/shard_map/dot_general | solution.py:521
Async XLA Ops:
  0.0 58.1 %copy-start = (bf16[1024,1024]{1,0:T(8,128)(2,1)S(1)}, bf16[1024,1024]{1,0:T(8,128)(2,1)}, u32[]{:S(2)}) copy-start(bf16[1024,1024]{1,0:T(8,128)(2,1)} %param.17) | copy-start | bytes 6291460

commit v5 on v4

--- a/solution.py
+++ b/solution.py
@@ -202,7 +202,7 @@
                     dst_ref[b, :, cols] = r[TOK * j : TOK * (j + 1)]
                 return 0
 
-            lax.fori_loop(0, D // 256, project, 0)
+            lax.fori_loop(0, D // 256, project, 0, unroll=UNROLL)
 
     half = iota((TOK, 128), 1) < 64
 
@@ -302,12 +302,11 @@
     for i in range(2):
         raw = pre_ref[i].astype(F32)
         own_ref[2 * g + i] = jnp.concatenate([raw[:, 0, :], raw[:, 1, :]], axis=1).astype(BF16)
-    table()
-    places()
     pl.semaphore_wait(barrier, len(greet))
 
     rows = [copy(own_ref.at[mine], own_ref.at[mine], device) for device in row_ids]
     back4 = copy(hid_ref, all_ref.at[0], tp_id(t + 4))
+    table()
     slides(0, TOK // 2)
     for c in rows:
         c.wait_recv()
@@ -415,29 +414,32 @@
             all_ref.at[3 - 2 * odd, parts[i]], all_ref.at[2, parts[i]], z_id(1 - 2 * odd)
         )
 
+    places()
     picks()
     run(0, "turn")
     run(1, "turn")
     norms(0)
+    projects((0,), [(wk_ref, k_ref), (wv_ref, v_ref)])
     run(0, "on", 0)
     run(0, "last")
     back2 = [two_back(0)]
+    suffix((0, 4), 0, 4, True, False)
     run(1, "on", 0)
     run(1, "last")
     back2.append(two_back(1))
+    suffix((0, 4), 4, 8, True, False)
+    run(0, "on", -1)
+    run(0, "on", 1)
     norms(1)
     norms(3)
-    projects((0, 1, 3), [(wk_ref, k_ref), (wv_ref, v_ref)])
-    run(0, "on", -1)
-    run(0, "on", 1)
-    suffix((0, 1, 3, 4), 0, 4, True, False)
+    projects((1, 3), [(wk_ref, k_ref), (wv_ref, v_ref)])
     run(1, "on", -1)
     run(1, "on", 1)
     run(0, "on", 2)
-    suffix((0, 1, 3, 4), 4, 8, True, False)
+    suffix((1, 3), 4, 8, False, False)
     run(1, "on", 2)
     run(0, "done")
-    prefix(0, (), False)
+    prefix(0, (1, 3), False)
     for c in back2:
         c.wait_recv()
     norms(2)

time: 60.8 us -> 57.6 us (0.947)
  Pallas kernels: 58.1 us -> 55.3 us
    pallas_call x1, Pallas kernels: 58.1 us -> 55.3 us  [layer(): pl.pallas_call(layer_kernel, out_shape=jax.ShapeDtypeStruct((TOK, D), BF1...]
where the time goes in v5:
time: 57.6 us; the launch traced here: 57.5 us
  Pallas kernels  55.3 us (96%)
  matrix products  2.1 us (4%)
    pallas_call x1, Pallas kernels, layer(): pl.pallas_call(layer_kernel, out_shape=jax.ShapeDtypeStruct((TOK, D), BF1...  55.3 us
    dot_general x1, matrix products, shards(): jnp.dot(mixed, w_out, preferred_element_type=jnp.float32)  2.1 us

profile of v5, /device:TPU:1, one launch (start us, length us, event | category | flops | bytes accessed | tf_op | source)
XLA Modules:
  0.0 57.5 jit_solution(6549963990648473975)
XLA Ops:
  0.0 0.0 copy-start
  0.0 55.3 %layer.1 = bf16[128,1024]{1,0:T(8,128)(2,1)} custom-call(s32[8]{0:T(128)} %slot_ref.1, bf16[128,1024]{1,0:T(8,128)(2,1)} %hid_ref.1, bf16[2,8,2,1024]{3,2,1,0:T(2,128)(2,1)} %pre_ref.1, bf16[8,128]{1,0:T(8,128)(2,1)} %bitcast.7, s32[8,128]{1,0:T(8,128)} %bitcast.6, f32[16,32]{1,0:T(8,128)} %bitcast.5, s32[1,128]{1,0:T(1,128)} %lens_ref.1, ...), custom_call_target="tpu_custom_call" | custom-call | tf_op jit(solution)/shard_map/layer/pallas_call | solution.py:459
  55.4 0.0 copy-done
  55.4 2.1 %convolution_convert_fusion = bf16[128,1024]{1,0:T(8,128)(2,1)} fusion(bf16[128,1024]{1,0:T(8,128)(2,1)} %layer.1, bf16[1024,1024]{1,0:T(8,128)(2,1)S(1)} %copy-done), kind=kOutput, calls=%fused_computation | convolution fusion | flops 268566528 | bytes 2621440 | tf_op jit(solution)/shard_map/dot_general | solution.py:523
Async XLA Ops:
  0.0 55.4 %copy-start = (bf16[1024,1024]{1,0:T(8,128)(2,1)S(1)}, bf16[1024,1024]{1,0:T(8,128)(2,1)}, u32[]{:S(2)}) copy-start(bf16[1024,1024]{1,0:T(8,128)(2,1)} %param.17) | copy-start | bytes 6291460

commit v6 on v5

--- a/solution.py
+++ b/solution.py
@@ -95,7 +95,9 @@
         used.append(out)
         return out
 
-    row_ids = [(lax.rem(g + d, 4), t) for d in (1, 2, 3)]
+    core = g % 2
+    away = 2 - 2 * (g // 2)
+    row_ids = [(away + core, t), (away + 1 - core, t), (g + 1 - 2 * core, t)]
     greet = row_ids + [tp_id(t + d) for d in (4, -4)]
     greet = greet + [ring(d) for ring in (x_id, y_id, z_id) for d in (1, -1)]
     barrier = pltpu.get_barrier_semaphore()

time: 57.6 us -> 57.6 us (level)
  no operation moved by 1% of the time
where the time goes in v6:
time: 57.6 us; the launch traced here: 57.5 us
  Pallas kernels  55.4 us (96%)
  matrix products  2.1 us (4%)
    pallas_call x1, Pallas kernels, layer(): pl.pallas_call(layer_kernel, out_shape=jax.ShapeDtypeStruct((TOK, D), BF1...  55.4 us
    dot_general x1, matrix products, shards(): jnp.dot(mixed, w_out, preferred_element_type=jnp.float32)  2.1 us

profile of v6, /device:TPU:1, one launch (start us, length us, event | category | flops | bytes accessed | tf_op | source)
XLA Modules:
  0.0 57.5 jit_solution(7793226741601349992)
XLA Ops:
  0.0 0.0 copy-start
  0.0 55.4 %layer.1 = bf16[128,1024]{1,0:T(8,128)(2,1)} custom-call(s32[8]{0:T(128)} %slot_ref.1, bf16[128,1024]{1,0:T(8,128)(2,1)} %hid_ref.1, bf16[2,8,2,1024]{3,2,1,0:T(2,128)(2,1)} %pre_ref.1, bf16[8,128]{1,0:T(8,128)(2,1)} %bitcast.7, s32[8,128]{1,0:T(8,128)} %bitcast.6, f32[16,32]{1,0:T(8,128)} %bitcast.5, s32[1,128]{1,0:T(1,128)} %lens_ref.1, ...), custom_call_target="tpu_custom_call" | custom-call | tf_op jit(solution)/shard_map/layer/pallas_call | solution.py:461
  55.4 0.0 copy-done
  55.4 2.1 %convolution_convert_fusion = bf16[128,1024]{1,0:T(8,128)(2,1)} fusion(bf16[128,1024]{1,0:T(8,128)(2,1)} %layer.1, bf16[1024,1024]{1,0:T(8,128)(2,1)S(1)} %copy-done), kind=kOutput, calls=%fused_computation | convolution fusion | flops 268566528 | bytes 2621440 | tf_op jit(solution)/shard_map/dot_general | solution.py:525
Async XLA Ops:
  0.0 55.4 %copy-start = (bf16[1024,1024]{1,0:T(8,128)(2,1)S(1)}, bf16[1024,1024]{1,0:T(8,128)(2,1)}, u32[]{:S(2)}) copy-start(bf16[1024,1024]{1,0:T(8,128)(2,1)} %param.17) | copy-start | bytes 6291460
